TPU v7x, 256 devices: a whole 4x4x8 slice. The times are simulated.
256 devices in a mesh: gen: 8 (over y, core), bus: 32 (over x, z).
Axes of the slice: x: 4, y: 4, z: 8, core: 2. Of those that a mesh axis runs over, the one named last changes fastest.
Arguments:
- bus_price: float32 [32, 12, 16384], P(None, None, 'bus'), may hold values from -4 to 4
- bus_demand: float32 [32, 12, 16384], P('gen', None, 'bus'), may hold values from 0 to 2
- multipliers: float32 [2, 32, 12, 24576], P(None, 'gen', None, 'bus'), may hold values from 0 to 1
- line_limits: float32 [24576], P('bus'), may hold values from 0.3 to 3
- ptdf_blocks: bfloat16 [192, 16, 128, 128], P('bus'), may hold values from -0.125 to 0.125
- ptdf_pattern: int32 [192, 16], P('bus'), may hold values from 0 to 127, as said below
- gen_bus: int32 [4096], P(('gen', 'bus')), may hold values from 0 to 16383, as said below
- state_counts: int32 [4096], P(('gen', 'bus')), may hold values from 64 to 512, as said below
- transitions: int32 [4096, 3, 512], P(('gen', 'bus')), may hold values from 0 to 511, as said below
- state_level: float32 [4096, 512], P(('gen', 'bus')), may hold values from 0 to 3
- state_cost: float32 [4096, 512], P(('gen', 'bus')), may hold values from 0 to 2
Outputs:
- new_multipliers: float32 [2, 32, 12, 24576], P(None, 'gen', None, 'bus')
- new_price: float32 [32, 12, 16384], P(None, None, 'bus')
Inputs may be any that keep to these rules, and one draw needn't show every extreme that they name: Generator i sits in bus block (i // 16) % 32: gen_bus[i] // 512 equals that number. `state_counts`: among the generators of each aligned group of 16, at most 6 have a count above 256, and some group has exactly 6. `transitions`: every successor of a state below its generator's count is below that count; a state at or above the count has itself as every successor. `ptdf_pattern`: the 16 bus blocks named in one row are different.
All inputs are finite; a program needn't handle non-finite values.
Results may differ from a plain program's by a relative error of at most 0.0031.
Values may be sent and summed in bfloat16 or wider, within the bound.
A program may use at most 128 MiB of HBM per device.

v0:
```python
import jax
import jax.numpy as jnp
from jax import lax
from jax.sharding import PartitionSpec as P

STATES = 512
BLK = 128
NNZB = 16


HIGHEST_PRECISION = lax.Precision.HIGHEST
STEP_SIZE = 1.0


def successor_matrix(trans_rows, state_span):
    columns = jnp.arange(state_span, dtype=jnp.int32)
    operator_table = jnp.zeros((trans_rows.shape[0], state_span, state_span), jnp.bfloat16)
    for branch in range(trans_rows.shape[1]):
        operator_table = operator_table + (
            trans_rows[:, branch, :state_span, None] == columns[None, None, :]
        ).astype(jnp.bfloat16)
    return operator_table


def smoothed_plan(level_rows, cost_rows, valid_rows, operator_table, hourly_prices):
    weights = valid_rows[None, :, None, :] * jnp.exp(
        hourly_prices[..., None] * level_rows[None, :, None, :] - cost_rows[None, :, None, :]
    )
    opening = weights[0] / jnp.sum(weights[0], axis=-1, keepdims=True)

    def forward(state_now, present_weight):
        pushed = jnp.einsum(
            "hkj,hjf->hkf",
            state_now.astype(jnp.bfloat16),
            operator_table,
            preferred_element_type=jnp.float32,
        )
        raised = pushed * present_weight
        scale_now = jnp.sum(raised, axis=-1, keepdims=True)
        state_next = raised / scale_now
        return (state_next, (state_next, scale_now))

    unused_state, (states_later, scales) = lax.scan(forward, opening, weights[1:])
    states_all = jnp.concatenate([opening[None], states_later], axis=0)

    def backward(back_now, inputs):
        present_weight, scale_now = inputs
        fetched_entries = (present_weight * back_now / scale_now).astype(jnp.bfloat16)
        back_prev = jnp.einsum(
            "fjc,fhc->fjh", fetched_entries, operator_table, preferred_element_type=jnp.float32
        )
        return (back_prev, back_prev)

    ones_back = jnp.ones_like(opening)
    unused_back, backs_earlier = lax.scan(backward, ones_back, (weights[1:], scales), reverse=True)
    backs_all = jnp.concatenate([backs_earlier, ones_back[None]], axis=0)
    combined_probability = states_all * backs_all
    return jnp.sum(combined_probability * level_rows[None, :, None, :], axis=-1) / jnp.sum(
        combined_probability, axis=-1
    )


def shards(
    bus_price,
    bus_demand,
    multipliers,
    line_limits,
    ptdf_blocks,
    ptdf_pattern,
    gen_bus,
    state_counts,
    transitions,
    state_level,
    state_cost,
):
    scn_all, hour_count, bus_dev = bus_price.shape
    scn_dev = bus_demand.shape[0]
    gen_index = lax.axis_index("gen")
    bus_index = lax.axis_index("bus")
    block_total = lax.axis_size("bus") * bus_dev // BLK
    local_bus = gen_bus - bus_index * bus_dev
    onehot_all = (local_bus[:, None] == jnp.arange(bus_dev, dtype=jnp.int32)[None, :]).astype(
        jnp.float32
    )
    valid_all = (jnp.arange(STATES, dtype=jnp.int32)[None, :] < state_counts[:, None]).astype(
        jnp.float32
    )
    operator_table = successor_matrix(transitions, STATES)
    hourly_prices = jnp.einsum("rtb,gb->tgr", bus_price, onehot_all, precision=HIGHEST_PRECISION)
    output = smoothed_plan(state_level, state_cost, valid_all, operator_table, hourly_prices)
    summed = jnp.einsum("tgr,gb->rtb", output, onehot_all, precision=HIGHEST_PRECISION)
    injections = lax.psum_scatter(summed, "gen", scatter_dimension=0, tiled=True)
    row_total = scn_dev * hour_count
    network_row_block = (injections - bus_demand).astype(jnp.bfloat16).reshape(row_total, bus_dev)
    line_blocks = ptdf_blocks.shape[0]
    wanted = ptdf_pattern.reshape(-1)
    piece_cols = lax.all_gather(network_row_block, "bus", axis=1, tiled=True)
    block_count = piece_cols.shape[1] // BLK
    block_ids = jnp.arange(block_count, dtype=jnp.int32)
    chooser = (wanted[:, None] == block_ids[None, :]).astype(jnp.bfloat16)
    blocked = piece_cols.reshape(piece_cols.shape[0], block_count, BLK)
    picked_blocks = jnp.einsum("rjb,mj->rmb", blocked, chooser, preferred_element_type=jnp.float32)
    gathered = picked_blocks.astype(jnp.bfloat16).reshape(row_total, line_blocks, NNZB, BLK)
    flows = jnp.einsum("rlkb,lkbc->rlc", gathered, ptdf_blocks, preferred_element_type=jnp.float32)
    flow_lines = flows.reshape(scn_dev, hour_count, line_blocks * BLK)
    upper_old = multipliers[0]
    lower_old = multipliers[1]
    upper_new = jnp.maximum(0.0, upper_old + STEP_SIZE * (flow_lines - line_limits[None, None, :]))
    lower_new = jnp.maximum(0.0, lower_old + STEP_SIZE * (-flow_lines - line_limits[None, None, :]))
    change = (
        (upper_new - upper_old - (lower_new - lower_old))
        .astype(jnp.bfloat16)
        .reshape(row_total, line_blocks, BLK)
    )
    spread = jnp.einsum("rlc,lkbc->rlkb", change, ptdf_blocks, preferred_element_type=jnp.float32)
    placing = (
        ptdf_pattern[:, :, None] == jnp.arange(block_total, dtype=jnp.int32)[None, None, :]
    ).astype(jnp.float32)
    partial_change = jnp.einsum(
        "rlkb,lkj->rjb", spread, placing, precision=HIGHEST_PRECISION
    ).reshape(scn_dev, hour_count, block_total * BLK)
    own_change = lax.psum_scatter(partial_change, "bus", scatter_dimension=2, tiled=True)
    own_price = lax.dynamic_slice_in_dim(bus_price, gen_index * scn_dev, scn_dev, 0)
    new_share = own_price - own_change
    new_price = lax.all_gather(new_share, "gen", axis=0, tiled=True)
    return (jnp.stack([upper_new, lower_new]), new_price)


def solution(mesh):
    in_specs = (
        P(None, None, "bus"),
        P("gen", None, "bus"),
        P(None, "gen", None, "bus"),
        P("bus"),
        P("bus", None, None, None),
        P("bus", None),
        P(("gen", "bus")),
        P(("gen", "bus")),
        P(("gen", "bus"), None, None),
        P(("gen", "bus"), None),
        P(("gen", "bus"), None),
    )
    out_specs = (P(None, "gen", None, "bus"), P(None, None, "bus"))
    return jax.shard_map(shards, mesh=mesh, in_specs=in_specs, out_specs=out_specs, check_vma=False)
```

profile of v0, /device:TPU:1, one launch (start us, length us, event | category | flops | bytes accessed | tf_op | source)
XLA Modules:
  0.0 687.4 jit_solution(12709552428947251052)
XLA Ops:
  8.8 2.0 convolution_bitcast_fusion.2
  10.8 3.3 exponential_multiply_fusion
  15.4 3.4 copy-done.1
  19.9 11.2 %slice.31 = f32[11,16,32,512]{3,2,1,0:T(8,128)} slice(f32[12,16,32,512]{3,2,1,0:T(8,128)} %copy-done.1), slice={[1:12], [0:16], [0:32], [0:512]} | slice | bytes 23068672 | tf_op jit(solution)/shard_map/slice | solution.py:43
  31.1 5.7 broadcast.49.clone
  36.8 103.0 %while.32 = (s32[]{:T(128)}, bf16[16,32,512]{2,1,0:T(8,128)(2,1)}, f32[11,16,32,512]{3,2,1,0:T(8,128)}, f32[11,16,32,1]{2,1,3,0:T(8,128)S(1)}, f32[11,16,32,512]...) while((s32[]{:T(128)}, bf16[16,32,512]{2,1,0:T(8,128)(2,1)}, ...), condition=%wide.region_3.4_spmd.clone, body=%wide.region_1.3_spmd.clone.sunk | while | flops 319815168 | bytes 5361777 | solution.py:43
  36.8 8.0 %fusion.75 = (f32[16,32]{1,0:T(8,128)S(1)}, f32[16,32,512]{2,1,0:T(8,128)S(1)}) fusion(f32[11,16,32,512]{3,2,1,0:T(8,128)} %get-tuple-element.389, s32[]{:T(128)S(6)} %copy.77, s32[16,512]{1,0:T(8,128)S(1)} %get-tuple-element.392, s32[16,512]{1,0:T(8,128)S(1)} %get-tuple-element.391, s32[16,512]{1,0:T(8,128)S(1)} %get-tuple-element.390, ...), kind=kOutput, calls=%fused_computation.83.clone.1 | convolution fusion | flops 319290880 | bytes 2721796 | tf_op jit(solution)/shard_map/while/body/eval_jaxpr/hkj,hjf->hkf/dot_general | solution.py:32
  44.8 1.3 bitcast_dynamic-update-slice_fusion.6
  46.2 8.0 %fusion.75 = (f32[16,32]{1,0:T(8,128)S(1)}, f32[16,32,512]{2,1,0:T(8,128)S(1)}) fusion(f32[11,16,32,512]{3,2,1,0:T(8,128)} %get-tuple-element.389, s32[]{:T(128)S(6)} %copy.77, s32[16,512]{1,0:T(8,128)S(1)} %get-tuple-element.392, s32[16,512]{1,0:T(8,128)S(1)} %get-tuple-element.391, s32[16,512]{1,0:T(8,128)S(1)} %get-tuple-element.390, ...), kind=kOutput, calls=%fused_computation.83.clone.1 | convolution fusion | flops 319290880 | bytes 2721796 | tf_op jit(solution)/shard_map/while/body/eval_jaxpr/hkj,hjf->hkf/dot_general | solution.py:32
  54.2 1.3 bitcast_dynamic-update-slice_fusion.6
  55.5 8.0 %fusion.75 = (f32[16,32]{1,0:T(8,128)S(1)}, f32[16,32,512]{2,1,0:T(8,128)S(1)}) fusion(f32[11,16,32,512]{3,2,1,0:T(8,128)} %get-tuple-element.389, s32[]{:T(128)S(6)} %copy.77, s32[16,512]{1,0:T(8,128)S(1)} %get-tuple-element.392, s32[16,512]{1,0:T(8,128)S(1)} %get-tuple-element.391, s32[16,512]{1,0:T(8,128)S(1)} %get-tuple-element.390, ...), kind=kOutput, calls=%fused_computation.83.clone.1 | convolution fusion | flops 319290880 | bytes 2721796 | tf_op jit(solution)/shard_map/while/body/eval_jaxpr/hkj,hjf->hkf/dot_general | solution.py:32
  63.6 1.3 bitcast_dynamic-update-slice_fusion.6
  64.9 8.0 %fusion.75 = (f32[16,32]{1,0:T(8,128)S(1)}, f32[16,32,512]{2,1,0:T(8,128)S(1)}) fusion(f32[11,16,32,512]{3,2,1,0:T(8,128)} %get-tuple-element.389, s32[]{:T(128)S(6)} %copy.77, s32[16,512]{1,0:T(8,128)S(1)} %get-tuple-element.392, s32[16,512]{1,0:T(8,128)S(1)} %get-tuple-element.391, s32[16,512]{1,0:T(8,128)S(1)} %get-tuple-element.390, ...), kind=kOutput, calls=%fused_computation.83.clone.1 | convolution fusion | flops 319290880 | bytes 2721796 | tf_op jit(solution)/shard_map/while/body/eval_jaxpr/hkj,hjf->hkf/dot_general | solution.py:32
  72.9 1.3 bitcast_dynamic-update-slice_fusion.6
  74.3 8.0 %fusion.75 = (f32[16,32]{1,0:T(8,128)S(1)}, f32[16,32,512]{2,1,0:T(8,128)S(1)}) fusion(f32[11,16,32,512]{3,2,1,0:T(8,128)} %get-tuple-element.389, s32[]{:T(128)S(6)} %copy.77, s32[16,512]{1,0:T(8,128)S(1)} %get-tuple-element.392, s32[16,512]{1,0:T(8,128)S(1)} %get-tuple-element.391, s32[16,512]{1,0:T(8,128)S(1)} %get-tuple-element.390, ...), kind=kOutput, calls=%fused_computation.83.clone.1 | convolution fusion | flops 319290880 | bytes 2721796 | tf_op jit(solution)/shard_map/while/body/eval_jaxpr/hkj,hjf->hkf/dot_general | solution.py:32
  82.3 1.3 bitcast_dynamic-update-slice_fusion.6
  83.6 8.0 %fusion.75 = (f32[16,32]{1,0:T(8,128)S(1)}, f32[16,32,512]{2,1,0:T(8,128)S(1)}) fusion(f32[11,16,32,512]{3,2,1,0:T(8,128)} %get-tuple-element.389, s32[]{:T(128)S(6)} %copy.77, s32[16,512]{1,0:T(8,128)S(1)} %get-tuple-element.392, s32[16,512]{1,0:T(8,128)S(1)} %get-tuple-element.391, s32[16,512]{1,0:T(8,128)S(1)} %get-tuple-element.390, ...), kind=kOutput, calls=%fused_computation.83.clone.1 | convolution fusion | flops 319290880 | bytes 2721796 | tf_op jit(solution)/shard_map/while/body/eval_jaxpr/hkj,hjf->hkf/dot_general | solution.py:32
  91.7 1.3 bitcast_dynamic-update-slice_fusion.6
  93.0 8.0 %fusion.75 = (f32[16,32]{1,0:T(8,128)S(1)}, f32[16,32,512]{2,1,0:T(8,128)S(1)}) fusion(f32[11,16,32,512]{3,2,1,0:T(8,128)} %get-tuple-element.389, s32[]{:T(128)S(6)} %copy.77, s32[16,512]{1,0:T(8,128)S(1)} %get-tuple-element.392, s32[16,512]{1,0:T(8,128)S(1)} %get-tuple-element.391, s32[16,512]{1,0:T(8,128)S(1)} %get-tuple-element.390, ...), kind=kOutput, calls=%fused_computation.83.clone.1 | convolution fusion | flops 319290880 | bytes 2721796 | tf_op jit(solution)/shard_map/while/body/eval_jaxpr/hkj,hjf->hkf/dot_general | solution.py:32
  101.0 1.3 bitcast_dynamic-update-slice_fusion.6
  102.4 8.0 %fusion.75 = (f32[16,32]{1,0:T(8,128)S(1)}, f32[16,32,512]{2,1,0:T(8,128)S(1)}) fusion(f32[11,16,32,512]{3,2,1,0:T(8,128)} %get-tuple-element.389, s32[]{:T(128)S(6)} %copy.77, s32[16,512]{1,0:T(8,128)S(1)} %get-tuple-element.392, s32[16,512]{1,0:T(8,128)S(1)} %get-tuple-element.391, s32[16,512]{1,0:T(8,128)S(1)} %get-tuple-element.390, ...), kind=kOutput, calls=%fused_computation.83.clone.1 | convolution fusion | flops 319290880 | bytes 2721796 | tf_op jit(solution)/shard_map/while/body/eval_jaxpr/hkj,hjf->hkf/dot_general | solution.py:32
  110.4 1.3 bitcast_dynamic-update-slice_fusion.6
  111.7 8.0 %fusion.75 = (f32[16,32]{1,0:T(8,128)S(1)}, f32[16,32,512]{2,1,0:T(8,128)S(1)}) fusion(f32[11,16,32,512]{3,2,1,0:T(8,128)} %get-tuple-element.389, s32[]{:T(128)S(6)} %copy.77, s32[16,512]{1,0:T(8,128)S(1)} %get-tuple-element.392, s32[16,512]{1,0:T(8,128)S(1)} %get-tuple-element.391, s32[16,512]{1,0:T(8,128)S(1)} %get-tuple-element.390, ...), kind=kOutput, calls=%fused_computation.83.clone.1 | convolution fusion | flops 319290880 | bytes 2721796 | tf_op jit(solution)/shard_map/while/body/eval_jaxpr/hkj,hjf->hkf/dot_general | solution.py:32
  119.8 1.3 bitcast_dynamic-update-slice_fusion.6
  121.1 8.0 %fusion.75 = (f32[16,32]{1,0:T(8,128)S(1)}, f32[16,32,512]{2,1,0:T(8,128)S(1)}) fusion(f32[11,16,32,512]{3,2,1,0:T(8,128)} %get-tuple-element.389, s32[]{:T(128)S(6)} %copy.77, s32[16,512]{1,0:T(8,128)S(1)} %get-tuple-element.392, s32[16,512]{1,0:T(8,128)S(1)} %get-tuple-element.391, s32[16,512]{1,0:T(8,128)S(1)} %get-tuple-element.390, ...), kind=kOutput, calls=%fused_computation.83.clone.1 | convolution fusion | flops 319290880 | bytes 2721796 | tf_op jit(solution)/shard_map/while/body/eval_jaxpr/hkj,hjf->hkf/dot_general | solution.py:32
  129.1 1.3 bitcast_dynamic-update-slice_fusion.6
  130.4 8.0 %fusion.75 = (f32[16,32]{1,0:T(8,128)S(1)}, f32[16,32,512]{2,1,0:T(8,128)S(1)}) fusion(f32[11,16,32,512]{3,2,1,0:T(8,128)} %get-tuple-element.389, s32[]{:T(128)S(6)} %copy.77, s32[16,512]{1,0:T(8,128)S(1)} %get-tuple-element.392, s32[16,512]{1,0:T(8,128)S(1)} %get-tuple-element.391, s32[16,512]{1,0:T(8,128)S(1)} %get-tuple-element.390, ...), kind=kOutput, calls=%fused_computation.83.clone.1 | convolution fusion | flops 319290880 | bytes 2721796 | tf_op jit(solution)/shard_map/while/body/eval_jaxpr/hkj,hjf->hkf/dot_general | solution.py:32
  138.5 1.3 bitcast_dynamic-update-slice_fusion.6
  140.9 5.8 broadcast.49
  146.8 118.3 %while.33 = (s32[]{:T(128)}, f32[16,32,512]{2,1,0:T(8,128)}, f32[11,16,32,512]{3,2,1,0:T(8,128)}, f32[11,16,32,512]{3,2,1,0:T(8,128)}, f32[11,16,32,1]{2,1,3,0:T...) while((s32[]{:T(128)}, f32[16,32,512]{2,1,0:T(8,128)}, ...), condition=%wide.region_5.6_spmd.clone, body=%wide.region_4.5_spmd.clone.sunk | while | flops 319553536 | bytes 6397045 | solution.py:55
  146.8 1.2 copy.96
  148.0 9.5 %bitcast_dynamic-update-slice_fusion.8 = (f32[11,16,32,512]{3,2,1,0:T(8,128)}, f32[16,32,512]{2,1,0:T(8,128)}) fusion(f32[11,16,32,512]{3,2,1,0:T(8,128)} %get-tuple-element.406, s32[]{:T(128)S(6)} %sub.131, s32[16,512]{1,0:T(8,128)S(1)} %get-tuple-element.421, s32[16,512]{1,0:T(8,128)S(1)} %get-tuple-element.420, ...), kind=kOutput, calls=%fused_computation.31.clone.1 | convolution fusion | flops 319553536 | bytes 4295680 | tf_op jit(solution)/shard_map/while/body/eval_jaxpr/fjc,fhc->fjh/dot_general | solution.py:49
  157.5 1.2 copy.96
  158.8 9.5 %bitcast_dynamic-update-slice_fusion.8 = (f32[11,16,32,512]{3,2,1,0:T(8,128)}, f32[16,32,512]{2,1,0:T(8,128)}) fusion(f32[11,16,32,512]{3,2,1,0:T(8,128)} %get-tuple-element.406, s32[]{:T(128)S(6)} %sub.131, s32[16,512]{1,0:T(8,128)S(1)} %get-tuple-element.421, s32[16,512]{1,0:T(8,128)S(1)} %get-tuple-element.420, ...), kind=kOutput, calls=%fused_computation.31.clone.1 | convolution fusion | flops 319553536 | bytes 4295680 | tf_op jit(solution)/shard_map/while/body/eval_jaxpr/fjc,fhc->fjh/dot_general | solution.py:49
  168.3 1.2 copy.96
  169.5 9.5 %bitcast_dynamic-update-slice_fusion.8 = (f32[11,16,32,512]{3,2,1,0:T(8,128)}, f32[16,32,512]{2,1,0:T(8,128)}) fusion(f32[11,16,32,512]{3,2,1,0:T(8,128)} %get-tuple-element.406, s32[]{:T(128)S(6)} %sub.131, s32[16,512]{1,0:T(8,128)S(1)} %get-tuple-element.421, s32[16,512]{1,0:T(8,128)S(1)} %get-tuple-element.420, ...), kind=kOutput, calls=%fused_computation.31.clone.1 | convolution fusion | flops 319553536 | bytes 4295680 | tf_op jit(solution)/shard_map/while/body/eval_jaxpr/fjc,fhc->fjh/dot_general | solution.py:49
  179.0 1.2 copy.96
  180.3 9.5 %bitcast_dynamic-update-slice_fusion.8 = (f32[11,16,32,512]{3,2,1,0:T(8,128)}, f32[16,32,512]{2,1,0:T(8,128)}) fusion(f32[11,16,32,512]{3,2,1,0:T(8,128)} %get-tuple-element.406, s32[]{:T(128)S(6)} %sub.131, s32[16,512]{1,0:T(8,128)S(1)} %get-tuple-element.421, s32[16,512]{1,0:T(8,128)S(1)} %get-tuple-element.420, ...), kind=kOutput, calls=%fused_computation.31.clone.1 | convolution fusion | flops 319553536 | bytes 4295680 | tf_op jit(solution)/shard_map/while/body/eval_jaxpr/fjc,fhc->fjh/dot_general | solution.py:49
  189.8 1.2 copy.96
  191.0 9.5 %bitcast_dynamic-update-slice_fusion.8 = (f32[11,16,32,512]{3,2,1,0:T(8,128)}, f32[16,32,512]{2,1,0:T(8,128)}) fusion(f32[11,16,32,512]{3,2,1,0:T(8,128)} %get-tuple-element.406, s32[]{:T(128)S(6)} %sub.131, s32[16,512]{1,0:T(8,128)S(1)} %get-tuple-element.421, s32[16,512]{1,0:T(8,128)S(1)} %get-tuple-element.420, ...), kind=kOutput, calls=%fused_computation.31.clone.1 | convolution fusion | flops 319553536 | bytes 4295680 | tf_op jit(solution)/shard_map/while/body/eval_jaxpr/fjc,fhc->fjh/dot_general | solution.py:49
  200.6 1.2 copy.96
  201.8 9.5 %bitcast_dynamic-update-slice_fusion.8 = (f32[11,16,32,512]{3,2,1,0:T(8,128)}, f32[16,32,512]{2,1,0:T(8,128)}) fusion(f32[11,16,32,512]{3,2,1,0:T(8,128)} %get-tuple-element.406, s32[]{:T(128)S(6)} %sub.131, s32[16,512]{1,0:T(8,128)S(1)} %get-tuple-element.421, s32[16,512]{1,0:T(8,128)S(1)} %get-tuple-element.420, ...), kind=kOutput, calls=%fused_computation.31.clone.1 | convolution fusion | flops 319553536 | bytes 4295680 | tf_op jit(solution)/shard_map/while/body/eval_jaxpr/fjc,fhc->fjh/dot_general | solution.py:49
  211.3 1.2 copy.96
  212.5 9.5 %bitcast_dynamic-update-slice_fusion.8 = (f32[11,16,32,512]{3,2,1,0:T(8,128)}, f32[16,32,512]{2,1,0:T(8,128)}) fusion(f32[11,16,32,512]{3,2,1,0:T(8,128)} %get-tuple-element.406, s32[]{:T(128)S(6)} %sub.131, s32[16,512]{1,0:T(8,128)S(1)} %get-tuple-element.421, s32[16,512]{1,0:T(8,128)S(1)} %get-tuple-element.420, ...), kind=kOutput, calls=%fused_computation.31.clone.1 | convolution fusion | flops 319553536 | bytes 4295680 | tf_op jit(solution)/shard_map/while/body/eval_jaxpr/fjc,fhc->fjh/dot_general | solution.py:49
  222.0 1.2 copy.96
  223.3 9.5 %bitcast_dynamic-update-slice_fusion.8 = (f32[11,16,32,512]{3,2,1,0:T(8,128)}, f32[16,32,512]{2,1,0:T(8,128)}) fusion(f32[11,16,32,512]{3,2,1,0:T(8,128)} %get-tuple-element.406, s32[]{:T(128)S(6)} %sub.131, s32[16,512]{1,0:T(8,128)S(1)} %get-tuple-element.421, s32[16,512]{1,0:T(8,128)S(1)} %get-tuple-element.420, ...), kind=kOutput, calls=%fused_computation.31.clone.1 | convolution fusion | flops 319553536 | bytes 4295680 | tf_op jit(solution)/shard_map/while/body/eval_jaxpr/fjc,fhc->fjh/dot_general | solution.py:49
  232.8 1.2 copy.96
  234.0 9.5 %bitcast_dynamic-update-slice_fusion.8 = (f32[11,16,32,512]{3,2,1,0:T(8,128)}, f32[16,32,512]{2,1,0:T(8,128)}) fusion(f32[11,16,32,512]{3,2,1,0:T(8,128)} %get-tuple-element.406, s32[]{:T(128)S(6)} %sub.131, s32[16,512]{1,0:T(8,128)S(1)} %get-tuple-element.421, s32[16,512]{1,0:T(8,128)S(1)} %get-tuple-element.420, ...), kind=kOutput, calls=%fused_computation.31.clone.1 | convolution fusion | flops 319553536 | bytes 4295680 | tf_op jit(solution)/shard_map/while/body/eval_jaxpr/fjc,fhc->fjh/dot_general | solution.py:49
  244.8 9.5 %bitcast_dynamic-update-slice_fusion.8 = (f32[11,16,32,512]{3,2,1,0:T(8,128)}, f32[16,32,512]{2,1,0:T(8,128)}) fusion(f32[11,16,32,512]{3,2,1,0:T(8,128)} %get-tuple-element.406, s32[]{:T(128)S(6)} %sub.131, s32[16,512]{1,0:T(8,128)S(1)} %get-tuple-element.421, s32[16,512]{1,0:T(8,128)S(1)} %get-tuple-element.420, ...), kind=kOutput, calls=%fused_computation.31.clone.1 | convolution fusion | flops 319553536 | bytes 4295680 | tf_op jit(solution)/shard_map/while/body/eval_jaxpr/fjc,fhc->fjh/dot_general | solution.py:49
  255.5 9.5 %bitcast_dynamic-update-slice_fusion.8 = (f32[11,16,32,512]{3,2,1,0:T(8,128)}, f32[16,32,512]{2,1,0:T(8,128)}) fusion(f32[11,16,32,512]{3,2,1,0:T(8,128)} %get-tuple-element.406, s32[]{:T(128)S(6)} %sub.131, s32[16,512]{1,0:T(8,128)S(1)} %get-tuple-element.421, s32[16,512]{1,0:T(8,128)S(1)} %get-tuple-element.420, ...), kind=kOutput, calls=%fused_computation.31.clone.1 | convolution fusion | flops 319553536 | bytes 4295680 | tf_op jit(solution)/shard_map/while/body/eval_jaxpr/fjc,fhc->fjh/dot_general | solution.py:49
  265.1 8.9 %fusion.37 = (f32[12,16,32]{2,1,0:T(8,128)S(1)}, f32[12,16,32]{2,1,0:T(8,128)S(1)}) fusion(f32[11,16,32,512]{3,2,1,0:T(8,128)} %get-tuple-element.159, f32[11,16,32,512]{3,2,1,0:T(8,128)} %get-tuple-element.157, f32[1,16,32,512]{3,2,1,0:T(8,128)} %slice_divide_fusion, f32[16,512]{1,0:T(8,128)S(1)} %copy-done.4), kind=kLoop, calls=%fused_computation.41 | loop fusion | flops 15716352 | bytes 24199168 | tf_op jit(solution)/shard_map/reduce_sum | solution.py:58
  273.9 1.4 convolution_bitcast_fusion.1
  276.7 67.6 %all-reduce.4.cloned.1.call-done = f32[32,12,512]{2,0,1:T(8,128)} async-done(((f32[32,12,512]{2,0,1:T(8,128)}), f32[32,12,512]{2,0,1:T(8,128)}) %all-reduce.4.cloned.1.call-update) | async-done | bytes 786448
  347.0 70.2 %all-gather.2.cloned.1.call-done = bf16[48,16384]{1,0:T(8,128)(2,1)} async-done(((bf16[48,512]{1,0:T(8,128)(2,1)}), bf16[48,16384]{1,0:T(8,128)(2,1)}) %all-gather.2.cloned.1.call-update) | async-done | bytes 1572880 | tf_op jit(solution)/shard_map/all_gather | solution.py:97
  417.2 1.8 copy.48
  422.0 1.9 add_maximum_fusion.1
  423.9 1.6 squeeze.27
  425.5 1.6 squeeze.26
  427.2 2.3 convolution_bitcast_fusion
  429.4 4.0 fusion.40
  433.4 3.7 reshape.84
  439.9 219.5 %reduce-scatter.3.cloned.1.call-done = f32[4,12,512]{2,1,0:T(8,128)} async-done(((f32[4,12,16384]{2,1,0:T(8,128)}), f32[4,12,512]{2,1,0:T(8,128)}) %reduce-scatter.3.cloned.1.call-update) | async-done | bytes 98320 | tf_op jit(solution)/shard_map/reduce_scatter | solution.py:122
  660.3 19.2 %all_gather.7 = f32[32,12,512]{2,1,0:T(8,128)S(1)} all-gather(f32[4,12,512]{2,1,0:T(8,128)S(1)} %copy_subtract_fusion), channel_id=1, replica_groups=mesh['gen'=8,'bus'=32] {'gen'}, dimensions={0}, use_global_device_ids=true | all-gather | bytes 884736 | tf_op jit(solution)/shard_map/all_gather | solution.py:125
  679.5 1.3 copy.39
  (69 shorter events, 17.8 us)
Async XLA Ops:
  7.2 412.3 %copy-start = (bf16[6,16,128,128]{3,2,1,0:T(8,128)(2,1)S(1)}, bf16[6,16,128,128]{3,2,1,0:T(8,128)(2,1)}, u32[]{:S(2)}) copy-start(bf16[6,16,128,128]{3,2,1,0:T(8,128)(2,1)} %param.19) | copy-start | bytes 9437188
  7.2 337.1 %all-reduce.4.cloned.1.call-start = ((), (), s32[]{:S(2)}) async-start(), calls=%async_computation.3 | async-start | bytes 1572864
  14.2 4.7 copy-start.1
  19.9 11.2 %copy-start.5 = (s32[16,3,512]{2,0,1:T(8,128)S(1)}, s32[16,3,512]{2,0,1:T(8,128)}, u32[]{:S(2)}) copy-start(s32[16,3,512]{2,0,1:T(8,128)} %param.23) | copy-start | bytes 294916
  146.8 118.3 %copy-start.4 = (f32[16,512]{1,0:T(8,128)S(1)}, f32[16,512]{1,0:T(8,128)}, u32[]{:S(2)}) copy-start(f32[16,512]{1,0:T(8,128)} %param.24) | copy-start | bytes 98308
  265.0 10.4 %copy-start.8 = (u32[256]{0:T(256)S(1)}, u32[256]{0:T(256)}, u32[]{:S(2)}) copy-start(u32[256]{0:T(256)} %constant.88) | copy-start | bytes 3076
  265.0 81.2 %copy-start.7 = (s32[6,16]{1,0:T(8,128)S(1)}, s32[6,16]{1,0:T(8,128)}, u32[]{:S(2)}) copy-start(s32[6,16]{1,0:T(8,128)} %param.20) | copy-start | bytes 1156
  265.0 81.2 %copy-start.3 = (f32[2,4,12,768]{3,1,2,0:T(4,128)S(1)}, f32[2,4,12,768]{3,1,2,0:T(4,128)}, u32[]{:S(2)}) copy-start(f32[2,4,12,768]{3,1,2,0:T(4,128)} %param.17) | copy-start | bytes 884740
  273.9 148.1 %copy-start.6 = (f32[768]{0:T(1024)S(1)}, f32[768]{0:T(1024)}, u32[]{:S(2)}) copy-start(f32[768]{0:T(1024)} %param.18) | copy-start | bytes 9220
  275.4 141.8 %all-gather.2.cloned.1.call-start = ((), (), s32[]{:S(2)}) async-start(), calls=%async_computation.1 | async-start | bytes 1622016 | tf_op jit(solution)/shard_map/all_gather | solution.py:97
  346.0 313.4 %reduce-scatter.3.cloned.1.call-start = ((), (), s32[]{:S(2)}) async-start(), calls=%async_computation.2 | async-start | bytes 4325376 | tf_op jit(solution)/shard_map/reduce_scatter | solution.py:122
  427.2 10.9 %copy-start.2 = (f32[1,4,12,768]{3,2,1,0:T(8,128)S(1)}, f32[1,4,12,768]{3,2,1,0:T(8,128)}, u32[]{:S(2)}) copy-start(f32[1,4,12,768]{3,2,1,0:T(8,128)} %get-tuple-element.248) | copy-start | bytes 442372
Sparse Core Ops, SparseCore 0:
  275.5 68.7 all-reduce.3
  347.3 69.8 all-gather.1
  437.2 222.1 reduce-scatter.2
where the time goes:
time: 692 us; the launch traced here: 687 us
  waiting for transfers between devices  357 us (52%)
  matrix products  204 us (29%)
  local copies, waits for them, and re-layouts  56.4 us (8%)
  other arithmetic  35.5 us (5%)
  blocking collectives  19.2 us (3%)
  between operations  14.6 us (2%)
    reduce_scatter x1, waiting for transfers between devices, shards(): lax.psum_scatter(partial_change, 'bus', scatter_dimension=2, tiled=True)  219 us
    dot_general x11, matrix products, backward(): jnp.einsum('fjc,fhc->fjh', fetched_entries, operator_table, preferred_ele...  105 us
    dot_general x11, matrix products, forward(): jnp.einsum('hkj,hjf->hkf', state_now.astype(jnp.bfloat16), operator_table...  88.4 us
    all_gather x1, waiting for transfers between devices, shards(): piece_cols = lax.all_gather(network_row_block, 'bus', axis=1, tiled=True)  70.2 us
    unnamed x4, waiting for transfers between devices  67.6 us
    all_gather x1, blocking collectives, shards(): new_price = lax.all_gather(new_share, 'gen', axis=0, tiled=True)  19.2 us
    dynamic_update_slice x11, other arithmetic, smoothed_plan(): lax.scan(forward, opening, weights[1:])  14.5 us
  transfers between devices with their start and end apart: 3, of which 3 were waited for; matrix products, arithmetic and copies ran while one was open for 1% of the time, Pallas kernels for 0%

commit v1 on v0

v1 whole, which is shorter than its diff:
```python
import functools

import jax
import jax.numpy as jnp
from jax import lax
from jax.experimental import pallas as pl
from jax.experimental.pallas import tpu as pltpu
from jax.sharding import PartitionSpec as P

STATES = 512
SMALL = 256
BIG_DEV = 6
GEN_DEV = 16
BLK = 128
NNZB = 16
HOURS = 12
SCN = 32
SCN_DEV = 4
ROWS = SCN_DEV * HOURS
BUS_DEV = 512
NX, NZ, NGEN = 4, 8, 8
LINE_BLKS = 6
F32, BF16, I32 = jnp.float32, jnp.bfloat16, jnp.int32
MESH = pl.DeviceIdType.MESH
NN = (((1,), (0,)), ((), ()))
NT = (((1,), (1,)), ((), ()))
VMEM_LIMIT = 58 * 1024 * 1024


def dot(a, b, dims):
    return lax.dot_general(a, b, dims, preferred_element_type=F32)


def split3(value):
    high = value.astype(BF16)
    rest = value - high.astype(F32)
    middle = rest.astype(BF16)
    low = (rest - middle.astype(F32)).astype(BF16)
    return high, middle, low


def plan_kernel(
    counts,
    gen_bus,
    trans,
    level,
    cost,
    price,
    out,
    order,
    padded,
    prices,
    levels,
    costs,
    op_big,
    op_small,
    fwd,
    bwd,
    fwd_now,
    bwd_now,
    result,
):
    base = lax.axis_index("gen") * GEN_DEV

    def place(g, big_so_far):
        big = (counts[g] > SMALL).astype(I32)
        slot = jnp.where(big == 1, big_so_far, GEN_DEV - 1 - (g - big_so_far))
        order[slot] = g
        return big_so_far + big

    lax.fori_loop(0, GEN_DEV, place, jnp.int32(0))

    lane = lax.broadcasted_iota(I32, (1, BLK), 1)
    offset_row = jnp.full((1, BLK), -1, I32)
    own_offsets = jnp.zeros((1, BLK), F32)
    for slot in range(GEN_DEV):
        offset = lax.rem(gen_bus[order[slot]], BUS_DEV)
        offset_row = jnp.where(lane == slot, offset, offset_row)
        own_offsets = jnp.where(lane == base + slot, offset.astype(F32), own_offsets)

    padded[:, HOURS:, :] = jnp.zeros((SCN, 16 - HOURS, BUS_DEV), F32)
    padded[:, :HOURS, :] = price[...]
    onehot = (lax.broadcasted_iota(I32, (BUS_DEV, BLK), 0) == offset_row).astype(BF16)
    pieces = split3(padded[...].reshape(SCN * 16, BUS_DEV))
    prices[...] = dot(pieces[0], onehot, NN) + dot(pieces[1], onehot, NN) + dot(pieces[2], onehot, NN)

    state_ids = lax.broadcasted_iota(I32, (1, STATES), 1)
    for slot in range(GEN_DEV):
        g = order[slot]
        levels[slot : slot + 1, :] = level[pl.ds(g, 1), :]
        costs[slot : slot + 1, :] = jnp.where(state_ids < counts[g], cost[pl.ds(g, 1), :], 1e4)

    chunk = 64
    for slot in range(GEN_DEV):
        g = order[slot]
        span = STATES if slot < BIG_DEV else SMALL
        table = op_big.at[slot] if slot < BIG_DEV else op_small.at[slot - BIG_DEV]
        targets = [trans[g, j : j + 1, :span] for j in range(3)]

        def build(part, carry, targets=targets, span=span, table=table):
            start = pl.multiple_of(part * chunk, chunk)
            ids = lax.broadcasted_iota(I32, (chunk, span), 0) + start
            hits = [jnp.where(target == ids, 1.0, 0.0) for target in targets]
            table[pl.ds(start, chunk), :] = (hits[0] + hits[1] + hits[2]).astype(BF16)
            return carry

        lax.fori_loop(0, span // chunk, build, 0)

    def span_of(slot):
        return STATES if slot < BIG_DEV else SMALL

    def operator(slot):
        return op_big[slot] if slot < BIG_DEV else op_small[slot - BIG_DEV]

    def hour_price(hour):
        return prices[pl.ds(hour, SCN, stride=16), :]

    def weight(slot, price_now):
        span = span_of(slot)
        return jnp.exp(
            price_now[:, slot : slot + 1] * levels[slot : slot + 1, :span] - costs[slot : slot + 1, :span]
        )

    def unit(value):
        return value * (1.0 / jnp.sum(value, axis=1, keepdims=True))

    def step_forward(slot, price_now):
        raised = dot(fwd_now[slot, :, : span_of(slot)], operator(slot), NT) * weight(slot, price_now)
        state = unit(raised)
        fwd_now[slot, :, : span_of(slot)] = state.astype(BF16)
        return state

    def step_backward(slot, price_now):
        back = dot(bwd_now[slot, :, : span_of(slot)], operator(slot), NN)
        bwd_now[slot, :, : span_of(slot)] = unit(back * weight(slot, price_now)).astype(BF16)
        return back

    first, last = hour_price(0), hour_price(HOURS - 1)
    for slot in range(GEN_DEV):
        span = span_of(slot)
        state = unit(weight(slot, first))
        fwd[0, slot, :, :span] = state
        fwd_now[slot, :, :span] = state.astype(BF16)
        bwd[0, slot, :, :span] = jnp.ones((SCN, span), F32)
        bwd_now[slot, :, :span] = unit(weight(slot, last)).astype(BF16)

    def early(k, carry):
        price_f, price_b = hour_price(k), hour_price(HOURS - 1 - k)
        for slot in range(GEN_DEV):
            span = span_of(slot)
            fwd[k, slot, :, :span] = step_forward(slot, price_f)
            bwd[k, slot, :, :span] = step_backward(slot, price_b)
        return carry

    lanes = lax.broadcasted_iota(I32, (SCN, BLK), 1) - base

    def mean_level(slot, state, back):
        combined = state * back
        span = span_of(slot)
        top = jnp.sum(combined * levels[slot : slot + 1, :span], axis=1, keepdims=True)
        return top / jnp.sum(combined, axis=1, keepdims=True)

    def late(k, carry):
        other = HOURS - 1 - k
        price_f, price_b = hour_price(k), hour_price(other)
        at_k = jnp.zeros((SCN, BLK), F32)
        at_other = jnp.zeros((SCN, BLK), F32)
        for slot in range(GEN_DEV):
            span = span_of(slot)
            state = step_forward(slot, price_f)
            back = step_backward(slot, price_b)
            at_k = jnp.where(lanes == slot, mean_level(slot, state, bwd[other, slot, :, :span]), at_k)
            at_other = jnp.where(lanes == slot, mean_level(slot, fwd[other, slot, :, :span], back), at_other)
        result[k] = at_k
        result[other] = at_other
        return carry

    half = HOURS // 2
    lax.fori_loop(1, half, early, 0)
    lax.fori_loop(half, HOURS, late, 0)

    for t in range(HOURS):
        out[pl.ds(t, SCN, stride=16), :] = result[t]
    out[pl.ds(HOURS, SCN, stride=16), :] = jnp.broadcast_to(own_offsets, (SCN, BLK))
    for t in range(HOURS + 1, 16):
        out[pl.ds(t, SCN, stride=16), :] = jnp.zeros((SCN, BLK), F32)


def plan(counts, gen_bus, trans, level, cost, price):
    vmem = pl.BlockSpec(memory_space=pltpu.VMEM)
    smem = pl.BlockSpec(memory_space=pltpu.SMEM)
    half = HOURS // 2
    return pl.pallas_call(
        plan_kernel,
        name="plan",
        out_shape=jax.ShapeDtypeStruct((SCN * 16, BLK), F32),
        in_specs=[smem, smem, vmem, vmem, vmem, vmem],
        out_specs=vmem,
        scratch_shapes=[
            pltpu.SMEM((GEN_DEV,), I32),
            pltpu.VMEM((SCN, 16, BUS_DEV), F32),
            pltpu.VMEM((SCN * 16, BLK), F32),
            pltpu.VMEM((GEN_DEV, STATES), F32),
            pltpu.VMEM((GEN_DEV, STATES), F32),
            pltpu.VMEM((BIG_DEV, STATES, STATES), BF16),
            pltpu.VMEM((GEN_DEV - BIG_DEV, SMALL, SMALL), BF16),
            pltpu.VMEM((half, GEN_DEV, SCN, STATES), F32),
            pltpu.VMEM((half, GEN_DEV, SCN, STATES), F32),
            pltpu.VMEM((GEN_DEV, SCN, STATES), BF16),
            pltpu.VMEM((GEN_DEV, SCN, STATES), BF16),
            pltpu.VMEM((HOURS, SCN, BLK), F32),
        ],
        compiler_params=pltpu.CompilerParams(vmem_limit_bytes=VMEM_LIMIT),
    )(counts, gen_bus, trans, level, cost, price)


class Links:
    def __init__(self, send, recv):
        self.send, self.recv, self.used, self.copies = send, recv, 0, {}
        self.x = lax.div(lax.axis_index("bus"), NZ)
        self.z = lax.rem(lax.axis_index("bus"), NZ)
        self.g = lax.axis_index("gen")

    def xs(self, step):
        return lax.rem(self.x + step + NX, NX)

    def zs(self, step):
        return lax.rem(self.z + step + NZ, NZ)

    def gs(self, step):
        return lax.rem(self.g + step + NGEN, NGEN)

    def along_x(self, step):
        return {"bus": self.xs(step) * NZ + self.z}

    def along_z(self, step):
        return {"bus": self.x * NZ + self.zs(step)}

    def along_gen(self, step):
        return {"gen": self.gs(step)}

    def start(self, key, src, dst, target):
        index = self.used
        self.used += 1
        copy = pltpu.make_async_remote_copy(
            src_ref=src,
            dst_ref=dst,
            send_sem=self.send.at[index],
            recv_sem=self.recv.at[index],
            device_id=target,
            device_id_type=MESH,
        )
        copy.start()
        self.copies[key] = copy

    def arrived(self, key):
        self.copies[key].wait_recv()

    def drain(self):
        for copy in self.copies.values():
            copy.wait_send()


def greet(targets):
    barrier = pltpu.get_barrier_semaphore()
    for target in targets:
        pl.semaphore_signal(barrier, inc=1, device_id=target, device_id_type=MESH)
    pl.semaphore_wait(barrier, len(targets))


def take_turns(*routines):
    waiting = list(routines)
    while waiting:
        for routine in list(waiting):
            if next(routine, "over") == "over":
                waiting.remove(routine)


def gather_z_first(net, buf):
    def block(dx, dz):
        return buf.at[net.xs(dx), net.zs(dz)]

    stages = [[0]] + [[-k, k] if k < NZ // 2 else [-k] for k in range(1, NZ // 2 + 1)]
    turn = 0
    for k, arrivals in enumerate(stages):
        for dz in arrivals:
            if k:
                net.arrived(("Az", dz))
            if dz <= 0 and k < NZ // 2:
                net.start(("Az", dz - 1), block(0, dz), block(0, dz), net.along_z(1))
            if dz >= 0 and k < NZ // 2 - 1:
                net.start(("Az", dz + 1), block(0, dz), block(0, dz), net.along_z(-1))
            net.start(("Ax", -1, dz), block(0, dz), block(0, dz), net.along_x(1))
            net.start(("Ax", 1, dz), block(0, dz), block(0, dz), net.along_x(-1))
        if k:
            for dz in stages[k - 1]:
                turn = relay(net, block, dz, turn)
        yield
    for dz in stages[-1]:
        turn = relay(net, block, dz, turn)
    yield
    for arrivals in stages:
        for dz in arrivals:
            net.arrived(("Ax", 2, dz))


def relay(net, block, dz, turn):
    net.arrived(("Ax", -1, dz))
    if turn == 0:
        net.start(("Ax", 2, dz), block(-1, dz), block(-1, dz), net.along_x(1))
    net.arrived(("Ax", 1, dz))
    if turn == 1:
        net.start(("Ax", 2, dz), block(1, dz), block(1, dz), net.along_x(-1))
    return 1 - turn


def gather_x_first(net, buf):
    def block(dx, dz):
        return buf.at[net.xs(dx), net.zs(dz)]

    def ring_step(dx, k):
        if k:
            net.arrived(("Bz", dx, -k))
        if k < NZ // 2:
            net.start(("Bz", dx, -k - 1), block(dx, -k), block(dx, -k), net.along_z(1))
        if 0 < k < NZ // 2:
            net.arrived(("Bz", dx, k))
        if k < NZ // 2 - 1:
            net.start(("Bz", dx, k + 1), block(dx, k), block(dx, k), net.along_z(-1))

    net.start(("Bx", -1), block(0, 0), block(0, 0), net.along_x(1))
    net.start(("Bx", 1), block(0, 0), block(0, 0), net.along_x(-1))
    ring_step(0, 0)
    yield
    net.arrived(("Bx", -1))
    net.start(("Bx", 2, 0), block(-1, 0).at[0], block(-1, 0).at[0], net.along_x(1))
    net.arrived(("Bx", 1))
    net.start(("Bx", 2, 1), block(1, 0).at[1], block(1, 0).at[1], net.along_x(-1))
    ring_step(-1, 0)
    ring_step(1, 0)
    ring_step(0, 1)
    yield
    net.arrived(("Bx", 2, 0))
    net.arrived(("Bx", 2, 1))
    ring_step(2, 0)
    for stage in range(2, NZ // 2 + 3):
        for dx, begin in ((0, 0), (-1, 1), (1, 1), (2, 2)):
            if 0 < stage - begin <= NZ // 2:
                ring_step(dx, stage - begin)
        yield


GATHER_COPIES = 7 + 31 + 32


def gather_kernel(generation, demand, out, own, peers, netf, buf, send, recv, done):
    net = Links(send, recv)
    neighbours = [net.along_x(1), net.along_x(-1), net.along_z(1), net.along_z(-1)]
    greet([net.along_gen(i) for i in range(1, NGEN)] + neighbours)

    share = SCN_DEV * 16
    for i in range(1, NGEN):
        src = generation.at[pl.ds(pl.multiple_of(net.gs(i) * share, share), share), :]
        net.start(("gen", i), src, peers.at[i], net.along_gen(i))
    total = generation[pl.ds(pl.multiple_of(net.g * share, share), share), :]
    for i in range(1, NGEN):
        net.arrived(("gen", i))
        total = total + peers[i]

    offsets = total[HOURS : HOURS + 1, :]
    spots = lax.broadcasted_iota(I32, (BUS_DEV, BLK), 0).astype(F32)
    onehot = (spots == offsets).astype(BF16)
    high, middle, low = split3(total)
    injections = dot(high, onehot, NT) + dot(middle, onehot, NT) + dot(low, onehot, NT)
    for n in range(SCN_DEV):
        netf[n * HOURS : (n + 1) * HOURS, :] = injections[n * 16 : n * 16 + HOURS, :] - demand[n]
    rounded = netf[...].astype(BF16)
    for half in range(2):
        for c in range(2):
            column = (half * 2 + c) * BLK
            buf[half, net.x, net.z, c] = rounded[:, column : column + BLK]

    take_turns(gather_z_first(net, buf.at[0]), gather_x_first(net, buf.at[1]))
    net.drain()
    copy = pltpu.make_async_copy(buf, out, done)
    copy.start()
    copy.wait()


def gather(generation, demand):
    vmem = pl.BlockSpec(memory_space=pltpu.VMEM)
    shape = (2, NX, NZ, 2, ROWS, BLK)
    return pl.pallas_call(
        gather_kernel,
        name="gather",
        out_shape=jax.ShapeDtypeStruct(shape, BF16),
        in_specs=[vmem, vmem],
        out_specs=pl.BlockSpec(memory_space=pl.ANY),
        scratch_shapes=[
            pltpu.VMEM((8, 128), F32),
            pltpu.VMEM((NGEN, SCN_DEV * 16, BLK), F32),
            pltpu.VMEM((ROWS, BUS_DEV), F32),
            pltpu.VMEM(shape, BF16),
            pltpu.SemaphoreType.DMA((GATHER_COPIES,)),
            pltpu.SemaphoreType.DMA((GATHER_COPIES,)),
            pltpu.SemaphoreType.DMA,
        ],
        compiler_params=pltpu.CompilerParams(
            collective_id=0, has_side_effects=True, vmem_limit_bytes=VMEM_LIMIT
        ),
    )(generation, demand)


def place_of(block):
    device, c = lax.div(block, 4), lax.rem(block, 4)
    return (lax.div(c, 2) * (NX * NZ) + device) * 2 + lax.rem(c, 2)


def flow_kernel(pattern, nets, ptdf, mult, limits, new_mult, shares, total, changes):
    total[...] = jnp.zeros(total.shape, F32)
    for line in range(LINE_BLKS):
        lanes = slice(line * BLK, (line + 1) * BLK)
        places = [place_of(pattern[line, j]) for j in range(NNZB)]
        flow = jnp.zeros((ROWS, BLK), F32)
        for j in range(0, NNZB, 2):
            pair = jnp.concatenate([nets[places[j]], nets[places[j + 1]]], axis=1)
            flow = flow + dot(pair, ptdf[line, j : j + 2].reshape(2 * BLK, BLK), NN)
        limit = limits[:, lanes]
        for n in range(SCN_DEV):
            here = flow[n * HOURS : (n + 1) * HOURS, :]
            upper_old, lower_old = mult[0, n, :, lanes], mult[1, n, :, lanes]
            upper = jnp.maximum(0.0, upper_old + (here - limit))
            lower = jnp.maximum(0.0, lower_old + (-here - limit))
            new_mult[0, n, :, lanes] = upper
            new_mult[1, n, :, lanes] = lower
            changes[n * HOURS : (n + 1) * HOURS, :] = (upper - upper_old) - (lower - lower_old)
        change = changes[...].astype(BF16)
        spread = dot(change, ptdf[line].reshape(NNZB * BLK, BLK), NT)
        for j in range(NNZB):
            total[places[j]] += spread[:, j * BLK : (j + 1) * BLK]
    shares[...] = total[...].astype(BF16)


def flows(pattern, nets, ptdf, mult, limits):
    vmem = pl.BlockSpec(memory_space=pltpu.VMEM)
    smem = pl.BlockSpec(memory_space=pltpu.SMEM)
    return pl.pallas_call(
        flow_kernel,
        name="flows",
        out_shape=(
            jax.ShapeDtypeStruct(mult.shape, F32),
            jax.ShapeDtypeStruct(nets.shape, BF16),
        ),
        in_specs=[smem, vmem, vmem, vmem, vmem],
        out_specs=(vmem, vmem),
        scratch_shapes=[
            pltpu.VMEM(nets.shape, F32),
            pltpu.VMEM((ROWS, BLK), F32),
        ],
        compiler_params=pltpu.CompilerParams(vmem_limit_bytes=VMEM_LIMIT),
    )(pattern, nets, ptdf, mult, limits)


def wide(value):
    return value.astype(F32)


def reduce_z_first(net, part, right, left, out_right, out_left, kept, sent, arrived, final):
    deep = NZ // 2
    columns = range(NX)
    for dx in columns:
        net.start(("Ar", 1, dx), part.at[net.xs(dx), net.zs(deep)], right.at[0, dx], net.along_z(1))
        net.start(("Al", 1, dx), part.at[net.xs(dx), net.zs(1 - deep)], left.at[0, dx], net.along_z(-1))
    yield
    for k in range(1, deep):
        for dx in columns:
            net.arrived(("Ar", k, dx))
            mine = part[net.xs(dx), net.zs(deep - k)]
            out_right[k - 1, dx] = (wide(right[k - 1, dx]) + wide(mine)).astype(BF16)
            net.start(("Ar", k + 1, dx), out_right.at[k - 1, dx], right.at[k, dx], net.along_z(1))
            if k < deep - 1:
                net.arrived(("Al", k, dx))
                mine = part[net.xs(dx), net.zs(1 - deep + k)]
                out_left[k - 1, dx] = (wide(left[k - 1, dx]) + wide(mine)).astype(BF16)
                net.start(("Al", k + 1, dx), out_left.at[k - 1, dx], left.at[k, dx], net.along_z(-1))
        yield
    for dx in (1, 2, 3, 0):
        net.arrived(("Al", deep - 1, dx))
        net.arrived(("Ar", deep, dx))
        value = wide(part[net.xs(dx), net.z]) + wide(right[deep - 1, dx]) + wide(left[deep - 2, dx])
        if dx:
            sent[dx] = value.astype(BF16)
            net.start(("Ax", dx), sent.at[dx], arrived.at[dx], net.along_x(dx))
        else:
            kept[...] = value
    yield
    value = kept[...]
    for dx in (1, 3, 2):
        net.arrived(("Ax", dx))
        value = value + wide(arrived[dx])
    final[...] = value.astype(BF16)
    yield from spread_result(net, 0)


def reduce_x_first(net, part, first, second, out_second, kept, sent, arrived, final):
    half = NZ // 2
    low, high = pl.ds(0, half), pl.ds(half, half)
    net.start(("B1", 0), part.at[net.xs(2), low], first.at[0], net.along_x(1))
    net.start(("B1", 1), part.at[net.xs(2), high], first.at[1], net.along_x(-1))
    net.start(("B2", 0, 1), part.at[net.xs(1), high], second.at[0, high], net.along_x(1))
    net.start(("B2", 1, 0), part.at[net.xs(-1), low], second.at[1, low], net.along_x(-1))
    yield
    net.arrived(("B1", 0))
    out_second[0] = (wide(first[0]) + wide(part[net.xs(1), low])).astype(BF16)
    net.start(("B2", 0, 0), out_second.at[0], second.at[0, low], net.along_x(1))
    net.arrived(("B1", 1))
    out_second[1] = (wide(first[1]) + wide(part[net.xs(-1), high])).astype(BF16)
    net.start(("B2", 1, 1), out_second.at[1], second.at[1, high], net.along_x(-1))
    yield
    for key in ((0, 1), (1, 0), (0, 0), (1, 1)):
        net.arrived(("B2",) + key)
    for dz in (4, 3, 5, 2, 6, 1, 7, 0):
        z = net.zs(dz)
        value = wide(part[net.x, z]) + wide(second[0, z]) + wide(second[1, z])
        if dz:
            sent[dz] = value.astype(BF16)
            net.start(("Bz", dz), sent.at[dz], arrived.at[dz], net.along_z(dz))
        else:
            kept[...] = value
    yield
    yield
    value = kept[...]
    for dz in (1, 7, 2, 6, 3, 5, 4):
        net.arrived(("Bz", dz))
        value = value + wide(arrived[dz])
    final[...] = value.astype(BF16)
    yield from spread_result(net, 1)


def spread_result(net, half):
    for i in range(1, NGEN):
        net.start(("gen", half, i), net.finals.at[0, half], net.finals.at[i, half], net.along_gen(i))
    yield


REDUCE_COPIES = 4 * 7 + 3 + 6 + 7 + 14


def reduce_kernel(
    shares,
    price,
    out,
    a_right,
    a_left,
    a_out_right,
    a_out_left,
    a_kept,
    a_sent,
    a_arrived,
    b_first,
    b_second,
    b_out,
    b_kept,
    b_sent,
    b_arrived,
    finals,
    send,
    recv,
):
    net = Links(send, recv)
    net.finals = finals
    greet(
        [net.along_x(i) for i in range(1, NX)]
        + [net.along_z(i) for i in range(1, NZ)]
        + [net.along_gen(i) for i in range(1, NGEN)]
    )
    take_turns(
        reduce_z_first(
            net, shares.at[0], a_right, a_left, a_out_right, a_out_left, a_kept, a_sent, a_arrived, finals.at[0, 0]
        ),
        reduce_x_first(net, shares.at[1], b_first, b_second, b_out, b_kept, b_sent, b_arrived, finals.at[0, 1]),
    )
    for i in range(NGEN):
        first = net.gs(-i) * SCN_DEV
        for half in range(2):
            if i:
                net.arrived(("gen", half, i))
            for c in range(2):
                columns = slice((half * 2 + c) * BLK, (half * 2 + c + 1) * BLK)
                change = wide(finals[i, half, c])
                for n in range(SCN_DEV):
                    out[first + n, :, columns] = (
                        price[first + n, :, columns] - change[n * HOURS : (n + 1) * HOURS, :]
                    )
    net.drain()


def reduce(shares, price):
    vmem = pl.BlockSpec(memory_space=pltpu.VMEM)
    piece = (2, ROWS, BLK)
    deep = NZ // 2
    return pl.pallas_call(
        reduce_kernel,
        name="reduce",
        out_shape=jax.ShapeDtypeStruct(price.shape, F32),
        in_specs=[vmem, vmem],
        out_specs=vmem,
        scratch_shapes=[
            pltpu.VMEM((deep, NX) + piece, BF16),
            pltpu.VMEM((deep - 1, NX) + piece, BF16),
            pltpu.VMEM((deep - 1, NX) + piece, BF16),
            pltpu.VMEM((deep - 2, NX) + piece, BF16),
            pltpu.VMEM(piece, F32),
            pltpu.VMEM((NX,) + piece, BF16),
            pltpu.VMEM((NX,) + piece, BF16),
            pltpu.VMEM((2, NZ // 2) + piece, BF16),
            pltpu.VMEM((2, NZ) + piece, BF16),
            pltpu.VMEM((2, NZ // 2) + piece, BF16),
            pltpu.VMEM(piece, F32),
            pltpu.VMEM((NZ,) + piece, BF16),
            pltpu.VMEM((NZ,) + piece, BF16),
            pltpu.VMEM((NGEN, 2) + piece, BF16),
            pltpu.SemaphoreType.DMA((REDUCE_COPIES,)),
            pltpu.SemaphoreType.DMA((REDUCE_COPIES,)),
        ],
        compiler_params=pltpu.CompilerParams(
            collective_id=1, has_side_effects=True, vmem_limit_bytes=VMEM_LIMIT
        ),
    )(shares, price)


def shards(
    bus_price,
    bus_demand,
    multipliers,
    line_limits,
    ptdf_blocks,
    ptdf_pattern,
    gen_bus,
    state_counts,
    transitions,
    state_level,
    state_cost,
):
    generation = plan(state_counts, gen_bus, transitions, state_level, state_cost, bus_price)
    nets = gather(generation, bus_demand)
    flat = (2 * NX * NZ * 2, ROWS, BLK)
    new_mult, shares = flows(
        ptdf_pattern, nets.reshape(flat), ptdf_blocks, multipliers, line_limits.reshape(1, -1)
    )
    new_price = reduce(shares.reshape(nets.shape), bus_price)
    return new_mult, new_price


def solution(mesh):
    in_specs = (
        P(None, None, "bus"),
        P("gen", None, "bus"),
        P(None, "gen", None, "bus"),
        P("bus"),
        P("bus", None, None, None),
        P("bus", None),
        P(("gen", "bus")),
        P(("gen", "bus")),
        P(("gen", "bus"), None, None),
        P(("gen", "bus"), None),
        P(("gen", "bus"), None),
    )
    out_specs = (P(None, "gen", None, "bus"), P(None, None, "bus"))
    return jax.shard_map(shards, mesh=mesh, in_specs=in_specs, out_specs=out_specs, check_vma=False)
```

time: 692 us -> 124 us (0.18)
  waiting for transfers between devices: 357 us -> 0 us
  matrix products: 204 us -> 0 us
  Pallas kernels: 0 us -> 110 us
  local copies, waits for them, and re-layouts: 56.4 us -> 12.2 us
  other arithmetic: 35.5 us -> 0 us
  blocking collectives: 19.2 us -> 0 us
  between operations: 14.6 us -> 0.66 us
    reduce_scatter x1 -> x0, waiting for transfers between devices: 219 us -> none  [shards(): lax.psum_scatter(partial_change, 'bus', scatter_dimension=2, tiled=True)]
    dot_general x28 -> x0, matrix products: 204 us -> none  [the longest x11 105 us: backward(): jnp.einsum('fjc,fhc->fjh', fetched_entries, operator_table, preferred_ele...]
    pallas_call x0 -> x4, Pallas kernels: none -> 110 us  [the longest x1 35.3 us: gather(): pl.pallas_call(gather_kernel, name='gather', out_shape=jax.ShapeDtypeStru...]
    all_gather x1 -> x0, waiting for transfers between devices: 70.2 us -> none  [shards(): piece_cols = lax.all_gather(network_row_block, 'bus', axis=1, tiled=True)]
    unnamed x4 -> x0, waiting for transfers between devices: 67.6 us -> none
    all_gather x1 -> x0, blocking collectives: 19.2 us -> none  [shards(): new_price = lax.all_gather(new_share, 'gen', axis=0, tiled=True)]
    dynamic_update_slice x11 -> x0, other arithmetic: 14.5 us -> none  [smoothed_plan(): lax.scan(forward, opening, weights[1:])]
    while x11 -> x0, local copies, waits for them, and re-layouts: 13.5 us -> none
  transfers between devices with their start and end apart: 3 -> 0, of which waited for: 3 -> 0; matrix products, arithmetic and copies ran while one was open for 1% -> 0% of each run, Pallas kernels for 0% -> 0%
where the time goes in v1:
time: 124 us; the launch traced here: 123 us
  Pallas kernels  110 us (89%)
  local copies, waits for them, and re-layouts  12.2 us (10%)
    pallas_call x1, Pallas kernels, gather(): pl.pallas_call(gather_kernel, name='gather', out_shape=jax.ShapeDtypeStru...  35.3 us
    pallas_call x1, Pallas kernels, reduce(): pl.pallas_call(reduce_kernel, name='reduce', out_shape=jax.ShapeDtypeStru...  34.6 us
    pallas_call x1, Pallas kernels, plan(): pl.pallas_call(plan_kernel, name='plan', out_shape=jax.ShapeDtypeStruct((...  34.3 us
    unnamed x8, local copies, waits for them, and re-layouts  10.8 us
    pallas_call x1, Pallas kernels, flows(): pl.pallas_call(flow_kernel, name='flows', out_shape=(jax.ShapeDtypeStruct...  6.2 us

profile of v1, /device:TPU:1, one launch (start us, length us, event | category | flops | bytes accessed | tf_op | source)
XLA Modules:
  0.0 123.2 jit_solution(5734521606147104421)
XLA Ops:
  0.6 0.0 copy-start
  0.6 1.3 %reshape.14.limits = f32[1,768]{1,0:T(1,128)} reshape(f32[768]{0:T(1024)} %param.14) | data formatting | bytes 6144 | tf_op jit(solution)/shard_map/reshape | solution.py:649
  2.0 1.6 %copy.15.demand = f32[4,12,512]{2,1,0:T(8,128)} copy(f32[4,12,512]{2,0,1:T(4,128)} %param.12) | data formatting | bytes 196608 | tf_op args[1]
  3.5 1.6 %copy.13.trans = s32[16,3,512]{2,1,0:T(4,128)} copy(s32[16,3,512]{2,0,1:T(8,128)} %param.19) | data formatting | bytes 196608 | tf_op args[8]
  5.1 1.8 %copy.16.mult = f32[2,4,12,768]{3,2,1,0:T(8,128)} copy(f32[2,4,12,768]{3,1,2,0:T(4,128)} %param.13) | data formatting | bytes 589824 | tf_op args[2]
  6.9 0.0 copy-done
  6.9 1.4 %copy.14.price = f32[32,12,512]{2,1,0:T(8,128)} copy(f32[32,12,512]{2,0,1:T(8,128)S(1)} %copy-done) | data formatting | bytes 1572864 | tf_op args[0]
  8.4 34.3 %plan.1.generation = f32[512,128]{1,0:T(8,128)} custom-call(s32[16]{0:T(128)} %counts.1, s32[16]{0:T(128)} %gen_bus.1, s32[16,3,512]{2,1,0:T(4,128)} %copy.13.trans, f32[16,512]{1,0:T(8,128)} %level.1, f32[16,512]{1,0:T(8,128)} %cost.1, f32[32,12,512]{2,1,0:T(8,128)} %copy.14.price), custom_call_target="tpu_custom_call" | custom-call | tf_op jit(solution)/shard_map/plan/pallas_call | solution.py:193
  42.7 35.3 %gather.1 = bf16[2,4,8,2,48,128]{5,4,3,2,1,0:T(8,128)(2,1)} custom-call(f32[512,128]{1,0:T(8,128)} %plan.1.generation, f32[4,12,512]{2,1,0:T(8,128)} %copy.15.demand), custom_call_target="tpu_custom_call" | custom-call | tf_op jit(solution)/shard_map/gather/pallas_call | solution.py:393
  77.9 6.2 %flows.1 = (f32[2,4,12,768]{3,2,1,0:T(8,128)}, bf16[128,48,128]{2,1,0:T(8,128)(2,1)}) custom-call(s32[6,16]{1,0:T(8,128)} %pattern.1, bf16[128,48,128]{2,1,0:T(8,128)(2,1)} %bitcast.2, bf16[6,16,128,128]{3,2,1,0:T(8,128)(2,1)} %ptdf.1, f32[2,4,12,768]{3,2,1,0:T(8,128)} %copy.16.mult, f32[1,768]{1,0:T(1,128)} %reshape.14.limits), custom_call_target="tpu_custom_call" | custom-call | tf_op jit(solution)/shard_map/flows/pallas_call | solution.py:447
  84.1 1.9 %copy.18 = f32[2,4,12,768]{3,1,2,0:T(4,128)} copy(f32[2,4,12,768]{3,2,1,0:T(8,128)} %get-tuple-element.6) | data formatting | bytes 589824
  86.0 34.6 %reduce.1 = f32[32,12,512]{2,1,0:T(8,128)} custom-call(bf16[2,4,8,2,48,128]{5,4,3,2,1,0:T(8,128)(2,1)} %bitcast.3, f32[32,12,512]{2,1,0:T(8,128)} %copy.14.price), custom_call_target="tpu_custom_call" | custom-call | tf_op jit(solution)/shard_map/reduce/pallas_call | solution.py:602
  120.6 2.6 %copy.19 = f32[32,12,512]{2,0,1:T(8,128)} copy(f32[32,12,512]{2,1,0:T(8,128)} %reduce.1) | data formatting | bytes 1572864
Async XLA Ops:
  0.6 6.3 %copy-start = (f32[32,12,512]{2,0,1:T(8,128)S(1)}, f32[32,12,512]{2,0,1:T(8,128)}, u32[]{:S(2)}) copy-start(f32[32,12,512]{2,0,1:T(8,128)} %param.11) | copy-start | bytes 2359300

commit v2 on v1

v2 whole, which is shorter than its diff:
```python
import functools

import jax
import jax.numpy as jnp
from jax import lax
from jax.experimental import pallas as pl
from jax.experimental.pallas import tpu as pltpu
from jax.sharding import PartitionSpec as P

STATES = 512
SMALL = 256
BIG_DEV = 6
GEN_DEV = 16
BLK = 128
NNZB = 16
HOURS = 12
SCN = 32
SCN_DEV = 4
ROWS = SCN_DEV * HOURS
BUS_DEV = 512
NX, NZ, NGEN = 4, 8, 8
LINE_BLKS = 6
F32, BF16, I32 = jnp.float32, jnp.bfloat16, jnp.int32
MESH = pl.DeviceIdType.MESH
NN = (((1,), (0,)), ((), ()))
NT = (((1,), (1,)), ((), ()))
OFFSET_LANE = (HOURS % 8) * GEN_DEV
VMEM_LIMIT = 58 * 1024 * 1024


def dot(a, b, dims):
    return lax.dot_general(a, b, dims, preferred_element_type=F32)


def split3(value):
    high = value.astype(BF16)
    rest = value - high.astype(F32)
    middle = rest.astype(BF16)
    low = (rest - middle.astype(F32)).astype(BF16)
    return high, middle, low


def plan_kernel(
    counts,
    gen_bus,
    pattern,
    trans,
    level,
    cost,
    price,
    out,
    inverse,
    order,
    prices,
    levels,
    costs,
    op_big,
    op_small,
    fwd,
    bwd,
    fwd_now,
    bwd_now,
    result,
):
    def place(g, big_so_far):
        big = (counts[g] > SMALL).astype(I32)
        slot = jnp.where(big == 1, big_so_far, GEN_DEV - 1 - (g - big_so_far))
        order[slot] = g
        return big_so_far + big

    lax.fori_loop(0, GEN_DEV, place, jnp.int32(0))

    def clear(block, carry):
        for line in range(LINE_BLKS):
            inverse[line, block] = LINE_BLKS * NNZB
        return carry

    def invert(j, carry):
        for line in range(LINE_BLKS):
            inverse[line, pattern[line, j]] = line * NNZB + j
        return carry

    lax.fori_loop(0, NX * NZ * 4, clear, 0)
    lax.fori_loop(0, NNZB, invert, 0)

    lane = lax.broadcasted_iota(I32, (1, BLK), 1)
    offset_row = jnp.full((1, BLK), -1, I32)
    sent_offsets = jnp.zeros((1, BLK), F32)
    for slot in range(GEN_DEV):
        offset = lax.rem(gen_bus[order[slot]], BUS_DEV)
        offset_row = jnp.where(lane == slot, offset, offset_row)
        sent_offsets = jnp.where(lane == OFFSET_LANE + slot, offset.astype(F32), sent_offsets)

    onehot = (lax.broadcasted_iota(I32, (BUS_DEV, BLK), 0) == offset_row).astype(BF16)
    pieces = split3(price[...].reshape(HOURS * SCN, BUS_DEV))
    prices[...] = dot(pieces[0], onehot, NN) + dot(pieces[1], onehot, NN) + dot(pieces[2], onehot, NN)

    state_ids = lax.broadcasted_iota(I32, (1, STATES), 1)
    for slot in range(GEN_DEV):
        g = order[slot]
        levels[slot : slot + 1, :] = level[pl.ds(g, 1), :]
        costs[slot : slot + 1, :] = jnp.where(state_ids < counts[g], cost[pl.ds(g, 1), :], 1e4)

    chunk = 64
    for slot in range(GEN_DEV):
        g = order[slot]
        span = STATES if slot < BIG_DEV else SMALL
        table = op_big.at[slot] if slot < BIG_DEV else op_small.at[slot - BIG_DEV]
        targets = [trans[j, pl.ds(g, 1), :span] for j in range(3)]

        def build(part, carry, targets=targets, span=span, table=table):
            start = pl.multiple_of(part * chunk, chunk)
            ids = lax.broadcasted_iota(I32, (chunk, span), 0) + start
            hits = [jnp.where(target == ids, 1.0, 0.0) for target in targets]
            table[pl.ds(start, chunk), :] = (hits[0] + hits[1] + hits[2]).astype(BF16)
            return carry

        lax.fori_loop(0, span // chunk, build, 0)

    def span_of(slot):
        return STATES if slot < BIG_DEV else SMALL

    def operator(slot):
        return op_big[slot] if slot < BIG_DEV else op_small[slot - BIG_DEV]

    def hour_price(hour):
        return prices[pl.ds(pl.multiple_of(hour * SCN, SCN), SCN), :]

    def weight(slot, price_now):
        span = span_of(slot)
        return jnp.exp(
            price_now[:, slot : slot + 1] * levels[slot : slot + 1, :span] - costs[slot : slot + 1, :span]
        )

    def unit(value):
        return value * (1.0 / jnp.sum(value, axis=1, keepdims=True))

    def step_forward(slot, price_now):
        raised = dot(fwd_now[slot, :, : span_of(slot)], operator(slot), NT) * weight(slot, price_now)
        state = unit(raised)
        fwd_now[slot, :, : span_of(slot)] = state.astype(BF16)
        return state

    def step_backward(slot, price_now):
        back = dot(bwd_now[slot, :, : span_of(slot)], operator(slot), NN)
        bwd_now[slot, :, : span_of(slot)] = unit(back * weight(slot, price_now)).astype(BF16)
        return back

    first, last = hour_price(0), hour_price(HOURS - 1)
    for slot in range(GEN_DEV):
        span = span_of(slot)
        state = unit(weight(slot, first))
        fwd[0, slot, :, :span] = state
        fwd_now[slot, :, :span] = state.astype(BF16)
        bwd[0, slot, :, :span] = jnp.ones((SCN, span), F32)
        bwd_now[slot, :, :span] = unit(weight(slot, last)).astype(BF16)

    def early(k, carry):
        price_f, price_b = hour_price(k), hour_price(HOURS - 1 - k)
        for slot in range(GEN_DEV):
            span = span_of(slot)
            fwd[k, slot, :, :span] = step_forward(slot, price_f)
            bwd[k, slot, :, :span] = step_backward(slot, price_b)
        return carry

    lanes = lax.broadcasted_iota(I32, (SCN, BLK), 1)

    def mean_level(slot, state, back):
        combined = state * back
        span = span_of(slot)
        top = jnp.sum(combined * levels[slot : slot + 1, :span], axis=1, keepdims=True)
        return top / jnp.sum(combined, axis=1, keepdims=True)

    result[0] = jnp.zeros((SCN, BLK), F32)
    result[1] = jnp.broadcast_to(sent_offsets, (SCN, BLK))

    def late(k, carry):
        other = HOURS - 1 - k
        price_f, price_b = hour_price(k), hour_price(other)
        at_k = jnp.zeros((SCN, BLK), F32)
        at_other = jnp.zeros((SCN, BLK), F32)
        lanes_k = lanes - lax.rem(k, 8) * GEN_DEV
        lanes_other = lanes - other * GEN_DEV
        for slot in range(GEN_DEV):
            span = span_of(slot)
            state = step_forward(slot, price_f)
            back = step_backward(slot, price_b)
            at_k = jnp.where(lanes_k == slot, mean_level(slot, state, bwd[other, slot, :, :span]), at_k)
            at_other = jnp.where(lanes_other == slot, mean_level(slot, fwd[other, slot, :, :span], back), at_other)
        result[lax.div(k, 8)] += at_k
        result[0] += at_other
        return carry

    half = HOURS // 2
    lax.fori_loop(1, half, early, 0)
    lax.fori_loop(half, HOURS, late, 0)

    for owner in range(NGEN):
        rows = slice(owner * SCN_DEV, (owner + 1) * SCN_DEV)
        for part in range(2):
            out[owner, part * SCN_DEV : (part + 1) * SCN_DEV, :] = result[part, rows, :]


def plan(counts, gen_bus, pattern, trans, level, cost, price):
    vmem = pl.BlockSpec(memory_space=pltpu.VMEM)
    smem = pl.BlockSpec(memory_space=pltpu.SMEM)
    half = HOURS // 2
    return pl.pallas_call(
        plan_kernel,
        name="plan",
        out_shape=(
            jax.ShapeDtypeStruct((NGEN, 2 * SCN_DEV, BLK), F32),
            jax.ShapeDtypeStruct((LINE_BLKS, NX * NZ * 4), I32),
        ),
        in_specs=[smem, smem, smem, vmem, vmem, vmem, vmem],
        out_specs=(vmem, smem),
        scratch_shapes=[
            pltpu.SMEM((GEN_DEV,), I32),
            pltpu.VMEM((HOURS * SCN, BLK), F32),
            pltpu.VMEM((GEN_DEV, STATES), F32),
            pltpu.VMEM((GEN_DEV, STATES), F32),
            pltpu.VMEM((BIG_DEV, STATES, STATES), BF16),
            pltpu.VMEM((GEN_DEV - BIG_DEV, SMALL, SMALL), BF16),
            pltpu.VMEM((half, GEN_DEV, SCN, STATES), F32),
            pltpu.VMEM((half, GEN_DEV, SCN, STATES), F32),
            pltpu.VMEM((GEN_DEV, SCN, STATES), BF16),
            pltpu.VMEM((GEN_DEV, SCN, STATES), BF16),
            pltpu.VMEM((2, SCN, BLK), F32),
        ],
        compiler_params=pltpu.CompilerParams(vmem_limit_bytes=VMEM_LIMIT),
    )(counts, gen_bus, pattern, trans, level, cost, price)


class Links:
    def __init__(self, send, recv):
        self.send, self.recv, self.used, self.copies = send, recv, 0, {}
        self.x = lax.div(lax.axis_index("bus"), NZ)
        self.z = lax.rem(lax.axis_index("bus"), NZ)
        self.g = lax.axis_index("gen")

    def xs(self, step):
        return lax.rem(self.x + step + NX, NX)

    def zs(self, step):
        return lax.rem(self.z + step + NZ, NZ)

    def gs(self, step):
        return lax.rem(self.g + step + NGEN, NGEN)

    def along_x(self, step):
        return {"bus": self.xs(step) * NZ + self.z}

    def along_z(self, step):
        return {"bus": self.x * NZ + self.zs(step)}

    def along_gen(self, step):
        return {"gen": self.gs(step)}

    def start(self, key, src, dst, target):
        index = self.used
        self.used += 1
        copy = pltpu.make_async_remote_copy(
            src_ref=src,
            dst_ref=dst,
            send_sem=self.send.at[index],
            recv_sem=self.recv.at[index],
            device_id=target,
            device_id_type=MESH,
        )
        copy.start()
        assert key not in self.copies
        self.copies[key] = copy

    def arrived(self, key):
        self.copies[key].wait_recv()

    def drain(self):
        for copy in self.copies.values():
            copy.wait_send()


def greet(targets):
    barrier = pltpu.get_barrier_semaphore()
    for target in targets:
        pl.semaphore_signal(barrier, inc=1, device_id=target, device_id_type=MESH)
    pl.semaphore_wait(barrier, len(targets))


def take_turns(*routines):
    waiting = list(routines)
    while waiting:
        for routine in list(waiting):
            if next(routine, "over") == "over":
                waiting.remove(routine)


def gather_z_first(net, buf):
    def block(dx, dz):
        return buf.at[net.xs(dx), net.zs(dz)]

    def pass_on(dz):
        for i in (1, -1, 2):
            net.start(("Ax", i, dz), block(0, dz), block(0, dz), net.along_x(i))

    for dz in (4, 3, -3, 2, -2, 1, -1):
        net.start(("Az", dz), block(0, 0), block(0, 0), net.along_z(dz))
    pass_on(0)
    yield
    for group in ((1, -1), (2, -2), (3, -3), (4,)):
        for dz in group:
            net.arrived(("Az", dz))
            pass_on(-dz)
        yield
    for dz in (0, -1, 1, -2, 2, -3, 3, -4):
        for i in (1, -1, 2):
            net.arrived(("Ax", i, dz))


def gather_x_first(net, buf):
    def block(dx, dz):
        return buf.at[net.xs(dx), net.zs(dz)]

    def first(dx):
        for i in (2, -2, 1, -1):
            net.start(("Bz", dx, i), block(dx, 0), block(dx, 0), net.along_z(i))

    def second(dx):
        for i in (2, -2):
            near = i // 2
            c = 0 if i > 0 else 1
            net.arrived(("Bz", dx, i))
            net.start(("Bz4", dx, i), block(dx, -i).at[c], block(dx, -i).at[c], net.along_z(i))
            net.start(("Bz3", dx, i), block(dx, -i), block(dx, -i), net.along_z(near))

    for i in (2, 1, -1):
        net.start(("Bx", i), block(0, 0), block(0, 0), net.along_x(i))
    first(0)
    yield
    for i in (-1, 1, 2):
        net.arrived(("Bx", i))
        first(-i)
    yield
    second(0)
    yield
    second(1)
    second(-1)
    yield
    second(-2)
    yield
    for dx in (0, 1, -1, -2):
        for i in (1, -1):
            net.arrived(("Bz", dx, i))
        for i in (2, -2):
            net.arrived(("Bz3", dx, i))
            net.arrived(("Bz4", dx, i))


def wide(value):
    return value.astype(F32)


def reduce_x_first(net, part, along_x, to_z, arrived, kept, final):
    far_first = (4, 3, 5, 2, 6, 1, 7, 0)
    for dz in far_first:
        for n, i in enumerate((2, 1, -1)):
            net.start(("sum Ax", n, dz), part.at[net.xs(i), net.zs(dz)], along_x.at[n, dz], net.along_x(i))
    yield
    yield
    for dz in far_first:
        value = wide(part[net.x, net.zs(dz)])
        for n in range(3):
            net.arrived(("sum Ax", n, dz))
            value = value + wide(along_x[n, dz])
        if dz:
            to_z[dz] = value.astype(BF16)
            net.start(("sum Az", dz), to_z.at[dz], arrived.at[dz], net.along_z(dz))
        else:
            kept[...] = value
        if dz in (5, 6):
            yield
    yield
    value = kept[...]
    for dz in (1, 7, 2, 6, 3, 5, 4):
        net.arrived(("sum Az", dz))
        value = value + wide(arrived[dz])
    final[...] = value.astype(BF16)
    yield from spread_result(net, 0)


def reduce_z_first(net, part, near, third, fourth, to_two, from_two, to_x, arrived, kept, final):
    columns = (2, 1, 3, 0)
    for dx in columns:
        column = net.xs(dx)
        for n, i in enumerate((1, -1)):
            net.start(("sum B4", dx, n), part.at[column, net.zs(4), n], fourth.at[dx, n], net.along_z(2 * i))
            net.start(("sum B3", dx, n), part.at[column, net.zs(3 * i)], third.at[dx, n], net.along_z(i))
    for dx in columns:
        for n, i in enumerate((1, -1)):
            net.start(("sum B1", dx, n), part.at[net.xs(dx), net.zs(i)], near.at[dx, n], net.along_z(i))
    yield
    for dx in columns:
        for n, i in enumerate((1, -1)):
            net.arrived(("sum B3", dx, n))
            net.arrived(("sum B4", dx, n))
            value = wide(part[net.xs(dx), net.zs(2 * i)]) + wide(third[dx, n])
            to_two[dx, n, 1 - n] = value[1 - n].astype(BF16)
            to_two[dx, n, n] = (value[n] + wide(fourth[dx, n])).astype(BF16)
            net.start(("sum B2", dx, n), to_two.at[dx, n], from_two.at[dx, n], net.along_z(2 * i))
        if dx in (2, 3):
            yield
    yield
    for dx in columns:
        value = wide(part[net.xs(dx), net.z])
        for n in range(2):
            net.arrived(("sum B1", dx, n))
            net.arrived(("sum B2", dx, n))
            value = value + (wide(near[dx, n]) + wide(from_two[dx, n]))
        if dx:
            to_x[dx] = value.astype(BF16)
            net.start(("sum Bx", dx), to_x.at[dx], arrived.at[dx], net.along_x(dx))
        else:
            kept[...] = value
    yield
    value = kept[...]
    for dx in (1, 3, 2):
        net.arrived(("sum Bx", dx))
        value = value + wide(arrived[dx])
    final[...] = value.astype(BF16)
    yield from spread_result(net, 1)


def spread_result(net, half):
    for i in range(1, NGEN):
        mine = net.finals.at[net.g, half]
        net.start(("out", half, i), mine, mine, net.along_gen(i))
    yield


NET_COPIES = 7 + 31 + 35 + 31 + 35 + 14


def place_of(block):
    device, c = lax.div(block, 4), lax.rem(block, 4)
    return (lax.div(c, 2) * (NX * NZ) + device) * 2 + lax.rem(c, 2)


def network_kernel(
    pattern,
    inverse,
    generation,
    demand,
    mult,
    limits,
    ptdf_far,
    price_far,
    new_price,
    new_mult,
    peers,
    netf,
    nets,
    ptdf,
    price,
    changes,
    spreads,
    shares,
    a_x,
    a_to_z,
    a_arrived,
    a_kept,
    b_near,
    b_third,
    b_fourth,
    b_to_two,
    b_from_two,
    b_to_x,
    b_arrived,
    b_kept,
    finals,
    send,
    recv,
    done,
):
    net = Links(send, recv)
    net.finals = finals
    load_ptdf = pltpu.make_async_copy(ptdf_far, ptdf, done.at[0])
    load_price = pltpu.make_async_copy(price_far, price, done.at[1])
    load_ptdf.start()
    load_price.start()
    greet(
        [net.along_x(i) for i in range(1, NX)]
        + [net.along_z(i) for i in range(1, NZ)]
        + [net.along_gen(i) for i in range(1, NGEN)]
    )

    for i in range(1, NGEN):
        net.start(("gen", i), generation.at[net.gs(i)], peers.at[net.g], net.along_gen(i))
    peers[net.g] = generation[net.g]
    for i in range(1, NGEN):
        net.arrived(("gen", i))
    lane_group = lax.div(lax.broadcasted_iota(I32, (2 * SCN_DEV, BLK), 1), GEN_DEV)
    by_hour = [jnp.zeros((2 * SCN_DEV, BLK), F32) for hour in range(8)]
    for source in range(NGEN):
        packed = peers[source]
        for hour in range(8):
            moved = pltpu.roll(packed, (source - hour) % NGEN * GEN_DEV, 1) if source != hour else packed
            by_hour[hour] = jnp.where(lane_group == source, moved, by_hour[hour])
    hours = [by_hour[t % 8][t // 8 * SCN_DEV : (t // 8 + 1) * SCN_DEV, :] for t in range(HOURS)]
    offsets = by_hour[HOURS % 8][SCN_DEV : SCN_DEV + 1, :]
    total = jnp.concatenate(hours, axis=0)

    spots = wide(lax.broadcasted_iota(I32, (BUS_DEV, BLK), 0))
    onehot = (spots == offsets).astype(BF16)
    high, middle, low = split3(total)
    netf[...] = dot(high, onehot, NT) + dot(middle, onehot, NT) + dot(low, onehot, NT)
    for t in range(HOURS):
        netf[t * SCN_DEV : (t + 1) * SCN_DEV, :] -= demand[t]
    rounded = netf[...].astype(BF16)
    for half in range(2):
        for c in range(2):
            column = (half * 2 + c) * BLK
            nets[half, net.x, net.z, c] = rounded[:, column : column + BLK]

    take_turns(gather_z_first(net, nets.at[0]), gather_x_first(net, nets.at[1]))

    load_ptdf.wait()
    blocks = nets.reshape(2 * NX * NZ * 2, ROWS, BLK)
    spreads[LINE_BLKS * NNZB] = jnp.zeros((ROWS, BLK), F32)
    for line in range(LINE_BLKS):
        lanes = slice(line * BLK, (line + 1) * BLK)
        places = [place_of(pattern[line, j]) for j in range(NNZB)]
        flow = jnp.zeros((ROWS, BLK), F32)
        for j in range(0, NNZB, 2):
            pair = jnp.concatenate([blocks[places[j]], blocks[places[j + 1]]], axis=1)
            flow = flow + dot(pair, ptdf[line, j : j + 2].reshape(2 * BLK, BLK), NN)
        limit = limits[:, lanes]
        for t in range(HOURS):
            rows = slice(t * SCN_DEV, (t + 1) * SCN_DEV)
            here = flow[rows, :]
            upper_old, lower_old = mult[0, t, :, lanes], mult[1, t, :, lanes]
            upper = jnp.maximum(0.0, upper_old + (here - limit))
            lower = jnp.maximum(0.0, lower_old + (-here - limit))
            new_mult[0, t, :, lanes] = upper
            new_mult[1, t, :, lanes] = lower
            changes[rows, :] = (upper - upper_old) - (lower - lower_old)
        change = changes[...].astype(BF16)
        spread = dot(change, ptdf[line].reshape(NNZB * BLK, BLK), NT)
        for j in range(NNZB):
            spreads[line * NNZB + j] = spread[:, j * BLK : (j + 1) * BLK]

    def collect(device, carry):
        x, z = lax.div(device, NZ), lax.rem(device, NZ)
        for half in range(2):
            for c in range(2):
                block = device * 4 + half * 2 + c
                value = spreads[inverse[0, block]]
                for line in range(1, LINE_BLKS):
                    value = value + spreads[inverse[line, block]]
                shares[half, x, z, c] = value.astype(BF16)
        return carry

    lax.fori_loop(0, NX * NZ, collect, 0)

    take_turns(
        reduce_x_first(net, shares.at[0], a_x, a_to_z, a_arrived, a_kept, finals.at[net.g, 0]),
        reduce_z_first(
            net,
            shares.at[1],
            b_near,
            b_third,
            b_fourth,
            b_to_two,
            b_from_two,
            b_to_x,
            b_arrived,
            b_kept,
            finals.at[net.g, 1],
        ),
    )
    load_price.wait()
    for half in range(2):
        for i in range(1, NGEN):
            net.arrived(("out", half, i))
        for owner in range(NGEN):
            scenarios = slice(owner * SCN_DEV, (owner + 1) * SCN_DEV)
            for c in range(2):
                columns = slice((half * 2 + c) * BLK, (half * 2 + c + 1) * BLK)
                change = wide(finals[owner, half, c])
                for t in range(HOURS):
                    new_price[t, scenarios, columns] = (
                        price[t, scenarios, columns] - change[t * SCN_DEV : (t + 1) * SCN_DEV, :]
                    )
    net.drain()


def network(pattern, inverse, generation, demand, mult, limits, ptdf, price):
    vmem = pl.BlockSpec(memory_space=pltpu.VMEM)
    smem = pl.BlockSpec(memory_space=pltpu.SMEM)
    far = pl.BlockSpec(memory_space=pl.ANY)
    piece = (2, ROWS, BLK)
    everything = (2, NX, NZ) + piece
    return pl.pallas_call(
        network_kernel,
        name="network",
        out_shape=(
            jax.ShapeDtypeStruct(price.shape, F32),
            jax.ShapeDtypeStruct(mult.shape, F32),
        ),
        in_specs=[smem, smem, vmem, vmem, vmem, vmem, far, far],
        out_specs=(vmem, vmem),
        scratch_shapes=[
            pltpu.VMEM(generation.shape, F32),
            pltpu.VMEM((ROWS, BUS_DEV), F32),
            pltpu.VMEM(everything, BF16),
            pltpu.VMEM(ptdf.shape, BF16),
            pltpu.VMEM(price.shape, F32),
            pltpu.VMEM((ROWS, BLK), F32),
            pltpu.VMEM((LINE_BLKS * NNZB + 1, ROWS, BLK), F32),
            pltpu.VMEM(everything, BF16),
            pltpu.VMEM((3, NZ) + piece, BF16),
            pltpu.VMEM((NZ,) + piece, BF16),
            pltpu.VMEM((NZ,) + piece, BF16),
            pltpu.VMEM(piece, F32),
            pltpu.VMEM((NX, 2) + piece, BF16),
            pltpu.VMEM((NX, 2) + piece, BF16),
            pltpu.VMEM((NX, 2, ROWS, BLK), BF16),
            pltpu.VMEM((NX, 2) + piece, BF16),
            pltpu.VMEM((NX, 2) + piece, BF16),
            pltpu.VMEM((NX,) + piece, BF16),
            pltpu.VMEM((NX,) + piece, BF16),
            pltpu.VMEM(piece, F32),
            pltpu.VMEM((NGEN, 2) + piece, BF16),
            pltpu.SemaphoreType.DMA((NET_COPIES,)),
            pltpu.SemaphoreType.DMA((NET_COPIES,)),
            pltpu.SemaphoreType.DMA((2,)),
        ],
        compiler_params=pltpu.CompilerParams(
            collective_id=0, has_side_effects=True, vmem_limit_bytes=VMEM_LIMIT
        ),
    )(pattern, inverse, generation, demand, mult, limits, ptdf, price)


def shards(
    bus_price,
    bus_demand,
    multipliers,
    line_limits,
    ptdf_blocks,
    ptdf_pattern,
    gen_bus,
    state_counts,
    transitions,
    state_level,
    state_cost,
):
    price = bus_price.transpose(1, 0, 2)
    generation, inverse = plan(
        state_counts, gen_bus, ptdf_pattern, transitions.transpose(1, 0, 2), state_level, state_cost, price
    )
    new_price, new_mult = network(
        ptdf_pattern,
        inverse,
        generation,
        bus_demand.transpose(1, 0, 2),
        multipliers.transpose(0, 2, 1, 3),
        line_limits.reshape(1, -1),
        ptdf_blocks,
        price,
    )
    return new_mult.transpose(0, 2, 1, 3), new_price.transpose(1, 0, 2)


def solution(mesh):
    in_specs = (
        P(None, None, "bus"),
        P("gen", None, "bus"),
        P(None, "gen", None, "bus"),
        P("bus"),
        P("bus", None, None, None),
        P("bus", None),
        P(("gen", "bus")),
        P(("gen", "bus")),
        P(("gen", "bus"), None, None),
        P(("gen", "bus"), None),
        P(("gen", "bus"), None),
    )
    out_specs = (P(None, "gen", None, "bus"), P(None, None, "bus"))
    return jax.shard_map(shards, mesh=mesh, in_specs=in_specs, out_specs=out_specs, check_vma=False)
```

time: 124 us -> 104 us (0.84)
  Pallas kernels: 110 us -> 97.9 us
  local copies, waits for them, and re-layouts: 12.2 us -> 5.04 us
    pallas_call x4 -> x2, Pallas kernels: 110 us -> 97.9 us  [the longest x1 62.6 us: network(): pl.pallas_call(network_kernel, name='network', out_shape=(jax.ShapeDtypeS...]
    unnamed x8 -> x2, local copies, waits for them, and re-layouts: 10.8 us -> 3.76 us
where the time goes in v2:
time: 104 us
  Pallas kernels  97.9 us (94%)
  local copies, waits for them, and re-layouts  5.04 us (5%)
    pallas_call x1, Pallas kernels, network(): pl.pallas_call(network_kernel, name='network', out_shape=(jax.ShapeDtypeS...  62.6 us
    pallas_call x1, Pallas kernels, plan(): pl.pallas_call(plan_kernel, name='plan', out_shape=(jax.ShapeDtypeStruct(...  35.3 us
    unnamed x2, local copies, waits for them, and re-layouts  3.76 us

profile of v2, /device:TPU:1, one launch (start us, length us, event | category | flops | bytes accessed | tf_op | source)
XLA Modules:
  0.0 103.6 jit_solution(5452434443265613224)
XLA Ops:
  0.6 1.3 %reshape.7.limits = f32[1,768]{1,0:T(1,128)} reshape(f32[768]{0:T(1024)} %param.14) | data formatting | bytes 6144 | tf_op jit(solution)/shard_map/reshape | solution.py:665
  1.9 35.3 %plan.1 = (f32[8,8,128]{2,1,0:T(8,128)}, s32[6,128]{1,0:T(8,128)}) custom-call(s32[16]{0:T(128)} %counts.1, s32[16]{0:T(128)} %gen_bus.1, s32[6,16]{1,0:T(8,128)} %pattern.3, s32[3,16,512]{2,1,0:T(8,128)} %bitcast.11, f32[16,512]{1,0:T(8,128)} %level.1, f32[16,512]{1,0:T(8,128)} %cost.1, f32[12,32,512]{2,1,0:T(8,128)} %bitcast.6), custom_call_target="tpu_custom_call" | custom-call | tf_op jit(solution)/shard_map/plan/pallas_call | solution.py:208
  37.2 62.6 %network.1 = (f32[12,32,512]{2,1,0:T(8,128)}, f32[2,12,4,768]{3,2,1,0:T(4,128)}) custom-call(s32[6,16]{1,0:T(8,128)} %pattern.3, s32[6,128]{1,0:T(8,128)} %get-tuple-element.6.inverse, f32[8,8,128]{2,1,0:T(8,128)} %get-tuple-element.7.generation, f32[12,4,512]{2,1,0:T(4,128)} %bitcast.12, f32[2,12,4,768]{3,2,1,0:T(4,128)} %bitcast.9, ...), custom_call_target="tpu_custom_call" | custom-call | tf_op jit(solution)/shard_map/network/pallas_call | solution.py:601
  99.8 1.7 %copy.15 = f32[2,4,12,768]{3,1,2,0:T(4,128)} copy(f32[2,4,12,768]{3,1,2,0:T(4,128)} %bitcast.10) | data formatting | bytes 589824
  101.5 2.1 %copy.16 = f32[32,12,512]{2,0,1:T(8,128)} copy(f32[32,12,512]{2,0,1:T(8,128)} %bitcast.8) | data formatting | bytes 1572864

commit v3 on v2

--- a/solution.py
+++ b/solution.py
@@ -56,6 +56,8 @@
     costs,
     op_big,
     op_small,
+    turned_big,
+    turned_small,
     fwd,
     bwd,
     fwd_now,
@@ -70,18 +72,15 @@
 
     lax.fori_loop(0, GEN_DEV, place, jnp.int32(0))
 
-    def clear(block, carry):
-        for line in range(LINE_BLKS):
+    def clear(line):
+        for block in range(NX * NZ * 4):
             inverse[line, block] = LINE_BLKS * NNZB
-        return carry
-
-    def invert(j, carry):
-        for line in range(LINE_BLKS):
+
+    def invert(line):
+        for j in range(NNZB):
             inverse[line, pattern[line, j]] = line * NNZB + j
-        return carry
-
-    lax.fori_loop(0, NX * NZ * 4, clear, 0)
-    lax.fori_loop(0, NNZB, invert, 0)
+
+    clear(0)
 
     lane = lax.broadcasted_iota(I32, (1, BLK), 1)
     offset_row = jnp.full((1, BLK), -1, I32)
@@ -101,18 +100,18 @@
         levels[slot : slot + 1, :] = level[pl.ds(g, 1), :]
         costs[slot : slot + 1, :] = jnp.where(state_ids < counts[g], cost[pl.ds(g, 1), :], 1e4)
 
-    chunk = 64
+    chunk = 256
     for slot in range(GEN_DEV):
         g = order[slot]
         span = STATES if slot < BIG_DEV else SMALL
         table = op_big.at[slot] if slot < BIG_DEV else op_small.at[slot - BIG_DEV]
-        targets = [trans[j, pl.ds(g, 1), :span] for j in range(3)]
+        targets = [trans[j, pl.ds(g, 1), :span].astype(jnp.int16) for j in range(3)]
 
         def build(part, carry, targets=targets, span=span, table=table):
             start = pl.multiple_of(part * chunk, chunk)
-            ids = lax.broadcasted_iota(I32, (chunk, span), 0) + start
-            hits = [jnp.where(target == ids, 1.0, 0.0) for target in targets]
-            table[pl.ds(start, chunk), :] = (hits[0] + hits[1] + hits[2]).astype(BF16)
+            ids = (lax.broadcasted_iota(I32, (chunk, span), 0) + start).astype(jnp.int16)
+            hits = [jnp.where(target == ids, BF16(1.0), BF16(0.0)) for target in targets]
+            table[pl.ds(start, chunk), :] = hits[0] + hits[1] + hits[2]
             return carry
 
         lax.fori_loop(0, span // chunk, build, 0)
@@ -122,6 +121,15 @@
 
     def operator(slot):
         return op_big[slot] if slot < BIG_DEV else op_small[slot - BIG_DEV]
+
+    def turned(slot):
+        return turned_big[slot] if slot < BIG_DEV else turned_small[slot - BIG_DEV]
+
+    def turn(slot):
+        if slot < BIG_DEV:
+            turned_big[slot] = op_big[slot].T
+        else:
+            turned_small[slot - BIG_DEV] = op_small[slot - BIG_DEV].T
 
     def hour_price(hour):
         return prices[pl.ds(pl.multiple_of(hour * SCN, SCN), SCN), :]
@@ -136,7 +144,7 @@
         return value * (1.0 / jnp.sum(value, axis=1, keepdims=True))
 
     def step_forward(slot, price_now):
-        raised = dot(fwd_now[slot, :, : span_of(slot)], operator(slot), NT) * weight(slot, price_now)
+        raised = dot(fwd_now[slot, :, : span_of(slot)], turned(slot), NN) * weight(slot, price_now)
         state = unit(raised)
         fwd_now[slot, :, : span_of(slot)] = state.astype(BF16)
         return state
@@ -149,6 +157,7 @@
     first, last = hour_price(0), hour_price(HOURS - 1)
     for slot in range(GEN_DEV):
         span = span_of(slot)
+        turn(slot)
         state = unit(weight(slot, first))
         fwd[0, slot, :, :span] = state
         fwd_now[slot, :, :span] = state.astype(BF16)
@@ -156,6 +165,7 @@
         bwd_now[slot, :, :span] = unit(weight(slot, last)).astype(BF16)
 
     def early(k, carry):
+        clear(k)
         price_f, price_b = hour_price(k), hour_price(HOURS - 1 - k)
         for slot in range(GEN_DEV):
             span = span_of(slot)
@@ -175,6 +185,7 @@
     result[1] = jnp.broadcast_to(sent_offsets, (SCN, BLK))
 
     def late(k, carry):
+        invert(k - HOURS // 2)
         other = HOURS - 1 - k
         price_f, price_b = hour_price(k), hour_price(other)
         at_k = jnp.zeros((SCN, BLK), F32)
@@ -221,6 +232,8 @@
             pltpu.VMEM((GEN_DEV, STATES), F32),
             pltpu.VMEM((BIG_DEV, STATES, STATES), BF16),
             pltpu.VMEM((GEN_DEV - BIG_DEV, SMALL, SMALL), BF16),
+            pltpu.VMEM((BIG_DEV, STATES, STATES), BF16),
+            pltpu.VMEM((GEN_DEV - BIG_DEV, SMALL, SMALL), BF16),
             pltpu.VMEM((half, GEN_DEV, SCN, STATES), F32),
             pltpu.VMEM((half, GEN_DEV, SCN, STATES), F32),
             pltpu.VMEM((GEN_DEV, SCN, STATES), BF16),
@@ -452,14 +465,12 @@
     mult,
     limits,
     ptdf_far,
-    price_far,
-    new_price,
+    finals,
     new_mult,
     peers,
     netf,
     nets,
     ptdf,
-    price,
     changes,
     spreads,
     shares,
@@ -475,17 +486,14 @@
     b_to_x,
     b_arrived,
     b_kept,
-    finals,
     send,
     recv,
     done,
 ):
     net = Links(send, recv)
     net.finals = finals
-    load_ptdf = pltpu.make_async_copy(ptdf_far, ptdf, done.at[0])
-    load_price = pltpu.make_async_copy(price_far, price, done.at[1])
+    load_ptdf = pltpu.make_async_copy(ptdf_far, ptdf, done)
     load_ptdf.start()
-    load_price.start()
     greet(
         [net.along_x(i) for i in range(1, NX)]
         + [net.along_z(i) for i in range(1, NZ)]
@@ -532,7 +540,7 @@
         for j in range(0, NNZB, 2):
             pair = jnp.concatenate([blocks[places[j]], blocks[places[j + 1]]], axis=1)
             flow = flow + dot(pair, ptdf[line, j : j + 2].reshape(2 * BLK, BLK), NN)
-        limit = limits[:, lanes]
+        limit = limits[lanes].reshape(1, BLK)
         for t in range(HOURS):
             rows = slice(t * SCN_DEV, (t + 1) * SCN_DEV)
             here = flow[rows, :]
@@ -576,23 +584,13 @@
             finals.at[net.g, 1],
         ),
     )
-    load_price.wait()
     for half in range(2):
         for i in range(1, NGEN):
             net.arrived(("out", half, i))
-        for owner in range(NGEN):
-            scenarios = slice(owner * SCN_DEV, (owner + 1) * SCN_DEV)
-            for c in range(2):
-                columns = slice((half * 2 + c) * BLK, (half * 2 + c + 1) * BLK)
-                change = wide(finals[owner, half, c])
-                for t in range(HOURS):
-                    new_price[t, scenarios, columns] = (
-                        price[t, scenarios, columns] - change[t * SCN_DEV : (t + 1) * SCN_DEV, :]
-                    )
     net.drain()
 
 
-def network(pattern, inverse, generation, demand, mult, limits, ptdf, price):
+def network(pattern, inverse, generation, demand, mult, limits, ptdf):
     vmem = pl.BlockSpec(memory_space=pltpu.VMEM)
     smem = pl.BlockSpec(memory_space=pltpu.SMEM)
     far = pl.BlockSpec(memory_space=pl.ANY)
@@ -602,17 +600,16 @@
         network_kernel,
         name="network",
         out_shape=(
-            jax.ShapeDtypeStruct(price.shape, F32),
+            jax.ShapeDtypeStruct((NGEN, 2) + piece, BF16),
             jax.ShapeDtypeStruct(mult.shape, F32),
         ),
-        in_specs=[smem, smem, vmem, vmem, vmem, vmem, far, far],
+        in_specs=[smem, smem, vmem, vmem, vmem, vmem, far],
         out_specs=(vmem, vmem),
         scratch_shapes=[
             pltpu.VMEM(generation.shape, F32),
             pltpu.VMEM((ROWS, BUS_DEV), F32),
             pltpu.VMEM(everything, BF16),
             pltpu.VMEM(ptdf.shape, BF16),
-            pltpu.VMEM(price.shape, F32),
             pltpu.VMEM((ROWS, BLK), F32),
             pltpu.VMEM((LINE_BLKS * NNZB + 1, ROWS, BLK), F32),
             pltpu.VMEM(everything, BF16),
@@ -628,15 +625,39 @@
             pltpu.VMEM((NX,) + piece, BF16),
             pltpu.VMEM((NX,) + piece, BF16),
             pltpu.VMEM(piece, F32),
-            pltpu.VMEM((NGEN, 2) + piece, BF16),
             pltpu.SemaphoreType.DMA((NET_COPIES,)),
             pltpu.SemaphoreType.DMA((NET_COPIES,)),
-            pltpu.SemaphoreType.DMA((2,)),
+            pltpu.SemaphoreType.DMA,
         ],
         compiler_params=pltpu.CompilerParams(
             collective_id=0, has_side_effects=True, vmem_limit_bytes=VMEM_LIMIT
         ),
-    )(pattern, inverse, generation, demand, mult, limits, ptdf, price)
+    )(pattern, inverse, generation, demand, mult, limits, ptdf)
+
+
+def finish_kernel(finals, price, mult, new_price, new_mult):
+    for owner in range(NGEN):
+        scenarios = slice(owner * SCN_DEV, (owner + 1) * SCN_DEV)
+        for block in range(4):
+            columns = slice(block * BLK, (block + 1) * BLK)
+            change = wide(finals[owner, block // 2, block % 2])
+            for t in range(HOURS):
+                new_price[t, scenarios, columns] = (
+                    price[t, scenarios, columns] - change[t * SCN_DEV : (t + 1) * SCN_DEV, :]
+                )
+    new_mult[...] = mult[...]
+
+
+def finish(finals, price, mult):
+    vmem = pl.BlockSpec(memory_space=pltpu.VMEM)
+    return pl.pallas_call(
+        finish_kernel,
+        name="finish",
+        out_shape=(jax.ShapeDtypeStruct(price.shape, F32), jax.ShapeDtypeStruct(mult.shape, F32)),
+        in_specs=[vmem] * 3,
+        out_specs=(vmem, vmem),
+        compiler_params=pltpu.CompilerParams(vmem_limit_bytes=VMEM_LIMIT),
+    )(finals, price, mult)
 
 
 def shards(
@@ -656,16 +677,16 @@
     generation, inverse = plan(
         state_counts, gen_bus, ptdf_pattern, transitions.transpose(1, 0, 2), state_level, state_cost, price
     )
-    new_price, new_mult = network(
+    finals, mult = network(
         ptdf_pattern,
         inverse,
         generation,
         bus_demand.transpose(1, 0, 2),
         multipliers.transpose(0, 2, 1, 3),
-        line_limits.reshape(1, -1),
+        line_limits,
         ptdf_blocks,
-        price,
     )
+    new_price, new_mult = finish(finals, price, mult)
     return new_mult.transpose(0, 2, 1, 3), new_price.transpose(1, 0, 2)
 
 

time: 104 us -> 93.5 us (0.90)
  Pallas kernels: 97.9 us -> 92.7 us
  local copies, waits for them, and re-layouts: 5.04 us -> 0 us
    pallas_call x1, Pallas kernels: 35.3 us -> 27.9 us  [plan(): pl.pallas_call(plan_kernel, name='plan', out_shape=(jax.ShapeDtypeStruct(...]
    unnamed x2 -> x0, local copies, waits for them, and re-layouts: 3.76 us -> none
    pallas_call x0 -> x1, Pallas kernels: none -> 2.48 us  [finish(): pl.pallas_call(finish_kernel, name='finish', out_shape=(jax.ShapeDtypeStr...]
    reshape x1 -> x0, local copies, waits for them, and re-layouts: 1.28 us -> none  [shards(): line_limits.reshape(1, -1)]
where the time goes in v3:
time: 93.5 us; the launch traced here: 93.3 us
  Pallas kernels  92.7 us (99%)
    pallas_call x1, Pallas kernels, network(): pl.pallas_call(network_kernel, name='network', out_shape=(jax.ShapeDtypeS...  62.3 us
    pallas_call x1, Pallas kernels, plan(): pl.pallas_call(plan_kernel, name='plan', out_shape=(jax.ShapeDtypeStruct(...  27.9 us
    pallas_call x1, Pallas kernels, finish(): pl.pallas_call(finish_kernel, name='finish', out_shape=(jax.ShapeDtypeStr...  2.48 us

profile of v3, /device:TPU:1, one launch (start us, length us, event | category | flops | bytes accessed | tf_op | source)
XLA Modules:
  0.0 93.3 jit_solution(16776739431123345590)
XLA Ops:
  0.6 27.9 %plan.1 = (f32[8,8,128]{2,1,0:T(8,128)}, s32[6,128]{1,0:T(8,128)}) custom-call(s32[16]{0:T(128)} %counts.1, s32[16]{0:T(128)} %gen_bus.1, s32[6,16]{1,0:T(8,128)} %pattern.3, s32[3,16,512]{2,1,0:T(8,128)} %bitcast.9, f32[16,512]{1,0:T(8,128)} %level.1, f32[16,512]{1,0:T(8,128)} %cost.1, f32[12,32,512]{2,1,0:T(8,128)} %bitcast.6), custom_call_target="tpu_custom_call" | custom-call | tf_op jit(solution)/shard_map/plan/pallas_call | solution.py:219
  28.5 62.3 %network.1 = (bf16[8,2,2,48,128]{4,3,2,1,0:T(8,128)(2,1)}, f32[2,12,4,768]{3,2,1,0:T(4,128)}) custom-call(s32[6,16]{1,0:T(8,128)} %pattern.3, s32[6,128]{1,0:T(8,128)} %get-tuple-element.8.inverse, f32[8,8,128]{2,1,0:T(8,128)} %get-tuple-element.9.generation, f32[12,4,512]{2,1,0:T(4,128)} %bitcast.10, f32[2,12,4,768]{3,2,1,0:T(4,128)} %bitcast.8, ...), custom_call_target="tpu_custom_call" | custom-call | tf_op jit(solution)/shard_map/network/pallas_call | solution.py:599
  90.9 2.5 %finish.1 = (f32[12,32,512]{2,1,0:T(8,128)}, f32[2,12,4,768]{3,2,1,0:T(4,128)}) custom-call(bf16[8,2,2,48,128]{4,3,2,1,0:T(8,128)(2,1)} %get-tuple-element.10.finals, f32[12,32,512]{2,1,0:T(8,128)} %bitcast.7, f32[2,12,4,768]{3,2,1,0:T(4,128)} %get-tuple-element.11.mult), custom_call_target="tpu_custom_call" | custom-call | tf_op jit(solution)/shard_map/finish/pallas_call | solution.py:653

commit v4 on v3

--- a/solution.py
+++ b/solution.py
@@ -40,7 +40,7 @@
     return high, middle, low
 
 
-def plan_kernel(
+def plan_steps(
     counts,
     gen_bus,
     pattern,
@@ -51,6 +51,8 @@
     out,
     inverse,
     order,
+    table_now,
+    table_done,
     prices,
     levels,
     costs,
@@ -64,23 +66,26 @@
     bwd_now,
     result,
 ):
-    def place(g, big_so_far):
+    big_so_far = jnp.int32(0)
+    slots = []
+    for g in range(GEN_DEV):
         big = (counts[g] > SMALL).astype(I32)
-        slot = jnp.where(big == 1, big_so_far, GEN_DEV - 1 - (g - big_so_far))
-        order[slot] = g
-        return big_so_far + big
-
-    lax.fori_loop(0, GEN_DEV, place, jnp.int32(0))
-
-    def clear(line):
-        for block in range(NX * NZ * 4):
-            inverse[line, block] = LINE_BLKS * NNZB
-
-    def invert(line):
+        slots.append(jnp.where(big == 1, big_so_far, GEN_DEV - 1 - (g - big_so_far)))
+        big_so_far = big_so_far + big
+    for slot in range(GEN_DEV):
+        holder = jnp.int32(0)
+        for g in range(1, GEN_DEV):
+            holder = holder + jnp.where(slots[g] == slot, g, 0)
+        order[slot] = holder
+
+    block_ids = lax.broadcasted_iota(I32, (1, NX * NZ * 4), 1)
+    for line in range(LINE_BLKS):
+        row = jnp.full((1, NX * NZ * 4), LINE_BLKS * NNZB, I32)
         for j in range(NNZB):
-            inverse[line, pattern[line, j]] = line * NNZB + j
-
-    clear(0)
+            row = jnp.where(block_ids == pattern[line, j], line * NNZB + j, row)
+        table_now[line : line + 1, :] = row
+    copy_table = pltpu.make_async_copy(table_now, inverse, table_done)
+    copy_table.start()
 
     lane = lax.broadcasted_iota(I32, (1, BLK), 1)
     offset_row = jnp.full((1, BLK), -1, I32)
@@ -165,7 +170,6 @@
         bwd_now[slot, :, :span] = unit(weight(slot, last)).astype(BF16)
 
     def early(k, carry):
-        clear(k)
         price_f, price_b = hour_price(k), hour_price(HOURS - 1 - k)
         for slot in range(GEN_DEV):
             span = span_of(slot)
@@ -185,7 +189,6 @@
     result[1] = jnp.broadcast_to(sent_offsets, (SCN, BLK))
 
     def late(k, carry):
-        invert(k - HOURS // 2)
         other = HOURS - 1 - k
         price_f, price_b = hour_price(k), hour_price(other)
         at_k = jnp.zeros((SCN, BLK), F32)
@@ -206,42 +209,34 @@
     lax.fori_loop(1, half, early, 0)
     lax.fori_loop(half, HOURS, late, 0)
 
+    copy_table.wait()
     for owner in range(NGEN):
         rows = slice(owner * SCN_DEV, (owner + 1) * SCN_DEV)
         for part in range(2):
             out[owner, part * SCN_DEV : (part + 1) * SCN_DEV, :] = result[part, rows, :]
 
 
-def plan(counts, gen_bus, pattern, trans, level, cost, price):
-    vmem = pl.BlockSpec(memory_space=pltpu.VMEM)
-    smem = pl.BlockSpec(memory_space=pltpu.SMEM)
+def plan_scratch():
     half = HOURS // 2
-    return pl.pallas_call(
-        plan_kernel,
-        name="plan",
-        out_shape=(
-            jax.ShapeDtypeStruct((NGEN, 2 * SCN_DEV, BLK), F32),
-            jax.ShapeDtypeStruct((LINE_BLKS, NX * NZ * 4), I32),
-        ),
-        in_specs=[smem, smem, smem, vmem, vmem, vmem, vmem],
-        out_specs=(vmem, smem),
-        scratch_shapes=[
-            pltpu.SMEM((GEN_DEV,), I32),
-            pltpu.VMEM((HOURS * SCN, BLK), F32),
-            pltpu.VMEM((GEN_DEV, STATES), F32),
-            pltpu.VMEM((GEN_DEV, STATES), F32),
-            pltpu.VMEM((BIG_DEV, STATES, STATES), BF16),
-            pltpu.VMEM((GEN_DEV - BIG_DEV, SMALL, SMALL), BF16),
-            pltpu.VMEM((BIG_DEV, STATES, STATES), BF16),
-            pltpu.VMEM((GEN_DEV - BIG_DEV, SMALL, SMALL), BF16),
-            pltpu.VMEM((half, GEN_DEV, SCN, STATES), F32),
-            pltpu.VMEM((half, GEN_DEV, SCN, STATES), F32),
-            pltpu.VMEM((GEN_DEV, SCN, STATES), BF16),
-            pltpu.VMEM((GEN_DEV, SCN, STATES), BF16),
-            pltpu.VMEM((2, SCN, BLK), F32),
-        ],
-        compiler_params=pltpu.CompilerParams(vmem_limit_bytes=VMEM_LIMIT),
-    )(counts, gen_bus, pattern, trans, level, cost, price)
+    return [
+        pltpu.VMEM((NGEN, 2 * SCN_DEV, BLK), F32),
+        pltpu.SMEM((8, NX * NZ * 4), I32),
+        pltpu.SMEM((GEN_DEV,), I32),
+        pltpu.VMEM((8, NX * NZ * 4), I32),
+        pltpu.SemaphoreType.DMA,
+        pltpu.VMEM((HOURS * SCN, BLK), F32),
+        pltpu.VMEM((GEN_DEV, STATES), F32),
+        pltpu.VMEM((GEN_DEV, STATES), F32),
+        pltpu.VMEM((BIG_DEV, STATES, STATES), BF16),
+        pltpu.VMEM((GEN_DEV - BIG_DEV, SMALL, SMALL), BF16),
+        pltpu.VMEM((BIG_DEV, STATES, STATES), BF16),
+        pltpu.VMEM((GEN_DEV - BIG_DEV, SMALL, SMALL), BF16),
+        pltpu.VMEM((half, GEN_DEV, SCN, STATES), F32),
+        pltpu.VMEM((half, GEN_DEV, SCN, STATES), F32),
+        pltpu.VMEM((GEN_DEV, SCN, STATES), BF16),
+        pltpu.VMEM((GEN_DEV, SCN, STATES), BF16),
+        pltpu.VMEM((2, SCN, BLK), F32),
+    ]
 
 
 class Links:
@@ -296,7 +291,7 @@
     barrier = pltpu.get_barrier_semaphore()
     for target in targets:
         pl.semaphore_signal(barrier, inc=1, device_id=target, device_id_type=MESH)
-    pl.semaphore_wait(barrier, len(targets))
+    return functools.partial(pl.semaphore_wait, barrier, len(targets))
 
 
 def take_turns(*routines):
@@ -458,9 +453,13 @@
 
 
 def network_kernel(
+    counts,
+    gen_bus,
     pattern,
-    inverse,
-    generation,
+    trans,
+    level,
+    cost,
+    price,
     demand,
     mult,
     limits,
@@ -489,16 +488,20 @@
     send,
     recv,
     done,
+    *plan_refs,
 ):
     net = Links(send, recv)
     net.finals = finals
     load_ptdf = pltpu.make_async_copy(ptdf_far, ptdf, done)
     load_ptdf.start()
-    greet(
+    everyone_here = greet(
         [net.along_x(i) for i in range(1, NX)]
         + [net.along_z(i) for i in range(1, NZ)]
         + [net.along_gen(i) for i in range(1, NGEN)]
     )
+    generation, inverse = plan_refs[0], plan_refs[1]
+    plan_steps(counts, gen_bus, pattern, trans, level, cost, price, *plan_refs)
+    everyone_here()
 
     for i in range(1, NGEN):
         net.start(("gen", i), generation.at[net.gs(i)], peers.at[net.g], net.along_gen(i))
@@ -555,42 +558,42 @@
         for j in range(NNZB):
             spreads[line * NNZB + j] = spread[:, j * BLK : (j + 1) * BLK]
 
-    def collect(device, carry):
+    def collect(half, device, carry):
         x, z = lax.div(device, NZ), lax.rem(device, NZ)
-        for half in range(2):
-            for c in range(2):
-                block = device * 4 + half * 2 + c
-                value = spreads[inverse[0, block]]
-                for line in range(1, LINE_BLKS):
-                    value = value + spreads[inverse[line, block]]
-                shares[half, x, z, c] = value.astype(BF16)
+        for c in range(2):
+            block = device * 4 + half * 2 + c
+            value = spreads[inverse[0, block]]
+            for line in range(1, LINE_BLKS):
+                value = value + spreads[inverse[line, block]]
+            shares[half, x, z, c] = value.astype(BF16)
         return carry
 
-    lax.fori_loop(0, NX * NZ, collect, 0)
-
-    take_turns(
-        reduce_x_first(net, shares.at[0], a_x, a_to_z, a_arrived, a_kept, finals.at[net.g, 0]),
-        reduce_z_first(
-            net,
-            shares.at[1],
-            b_near,
-            b_third,
-            b_fourth,
-            b_to_two,
-            b_from_two,
-            b_to_x,
-            b_arrived,
-            b_kept,
-            finals.at[net.g, 1],
-        ),
+    lax.fori_loop(0, NX * NZ, functools.partial(collect, 1), 0)
+    longer = reduce_z_first(
+        net,
+        shares.at[1],
+        b_near,
+        b_third,
+        b_fourth,
+        b_to_two,
+        b_from_two,
+        b_to_x,
+        b_arrived,
+        b_kept,
+        finals.at[net.g, 1],
     )
+    next(longer)
+    lax.fori_loop(0, NX * NZ, functools.partial(collect, 0), 0)
+    shorter = reduce_x_first(net, shares.at[0], a_x, a_to_z, a_arrived, a_kept, finals.at[net.g, 0])
+    next(shorter)
+    take_turns(longer, shorter)
     for half in range(2):
         for i in range(1, NGEN):
             net.arrived(("out", half, i))
     net.drain()
 
 
-def network(pattern, inverse, generation, demand, mult, limits, ptdf):
+def network(counts, gen_bus, pattern, trans, level, cost, price, demand, mult, limits, ptdf):
     vmem = pl.BlockSpec(memory_space=pltpu.VMEM)
     smem = pl.BlockSpec(memory_space=pltpu.SMEM)
     far = pl.BlockSpec(memory_space=pl.ANY)
@@ -603,10 +606,10 @@
             jax.ShapeDtypeStruct((NGEN, 2) + piece, BF16),
             jax.ShapeDtypeStruct(mult.shape, F32),
         ),
-        in_specs=[smem, smem, vmem, vmem, vmem, vmem, far],
+        in_specs=[smem] * 3 + [vmem] * 7 + [far],
         out_specs=(vmem, vmem),
         scratch_shapes=[
-            pltpu.VMEM(generation.shape, F32),
+            pltpu.VMEM((NGEN, 2 * SCN_DEV, BLK), F32),
             pltpu.VMEM((ROWS, BUS_DEV), F32),
             pltpu.VMEM(everything, BF16),
             pltpu.VMEM(ptdf.shape, BF16),
@@ -628,11 +631,12 @@
             pltpu.SemaphoreType.DMA((NET_COPIES,)),
             pltpu.SemaphoreType.DMA((NET_COPIES,)),
             pltpu.SemaphoreType.DMA,
-        ],
+        ]
+        + plan_scratch(),
         compiler_params=pltpu.CompilerParams(
             collective_id=0, has_side_effects=True, vmem_limit_bytes=VMEM_LIMIT
         ),
-    )(pattern, inverse, generation, demand, mult, limits, ptdf)
+    )(counts, gen_bus, pattern, trans, level, cost, price, demand, mult, limits, ptdf)
 
 
 def finish_kernel(finals, price, mult, new_price, new_mult):
@@ -674,13 +678,14 @@
     state_cost,
 ):
     price = bus_price.transpose(1, 0, 2)
-    generation, inverse = plan(
-        state_counts, gen_bus, ptdf_pattern, transitions.transpose(1, 0, 2), state_level, state_cost, price
-    )
     finals, mult = network(
+        state_counts,
+        gen_bus,
         ptdf_pattern,
-        inverse,
-        generation,
+        transitions.transpose(1, 0, 2),
+        state_level,
+        state_cost,
+        price,
         bus_demand.transpose(1, 0, 2),
         multipliers.transpose(0, 2, 1, 3),
         line_limits,

time: 93.5 us -> 89.6 us (0.958)
  Pallas kernels: 92.7 us -> 88.7 us
    pallas_call x1 -> x0, Pallas kernels: 27.9 us -> none  [plan(): pl.pallas_call(plan_kernel, name='plan', out_shape=(jax.ShapeDtypeStruct(...]
    pallas_call x1, Pallas kernels: 62.3 us -> 86.2 us  [network(): pl.pallas_call(network_kernel, name='network', out_shape=(jax.ShapeDtypeS...]
where the time goes in v4:
time: 89.6 us; the launch traced here: 89.3 us
  Pallas kernels  88.7 us (99%)
    pallas_call x1, Pallas kernels, network(): pl.pallas_call(network_kernel, name='network', out_shape=(jax.ShapeDtypeS...  86.2 us
    pallas_call x1, Pallas kernels, finish(): pl.pallas_call(finish_kernel, name='finish', out_shape=(jax.ShapeDtypeStr...  2.48 us

profile of v4, /device:TPU:1, one launch (start us, length us, event | category | flops | bytes accessed | tf_op | source)
XLA Modules:
  0.0 89.3 jit_solution(2827533614817343329)
XLA Ops:
  0.6 86.2 %network.1 = (bf16[8,2,2,48,128]{4,3,2,1,0:T(8,128)(2,1)}, f32[2,12,4,768]{3,2,1,0:T(4,128)}) custom-call(s32[16]{0:T(128)} %counts.1, s32[16]{0:T(128)} %gen_bus.1, s32[6,16]{1,0:T(8,128)} %pattern.1, s32[3,16,512]{2,1,0:T(8,128)} %bitcast.9, f32[16,512]{1,0:T(8,128)} %level.1, f32[16,512]{1,0:T(8,128)} %cost.1, f32[12,32,512]{2,1,0:T(8,128)} %bitcast.6, ...), custom_call_target="tpu_custom_call" | custom-call | tf_op jit(solution)/shard_map/network/pallas_call | solution.py:602
  86.8 2.5 %finish.1 = (f32[12,32,512]{2,1,0:T(8,128)}, f32[2,12,4,768]{3,2,1,0:T(4,128)}) custom-call(bf16[8,2,2,48,128]{4,3,2,1,0:T(8,128)(2,1)} %get-tuple-element.6.finals, f32[12,32,512]{2,1,0:T(8,128)} %bitcast.7, f32[2,12,4,768]{3,2,1,0:T(4,128)} %get-tuple-element.7.mult), custom_call_target="tpu_custom_call" | custom-call | tf_op jit(solution)/shard_map/finish/pallas_call | solution.py:657

commit v5 on v4

--- a/solution.py
+++ b/solution.py
@@ -310,7 +310,7 @@
         for i in (1, -1, 2):
             net.start(("Ax", i, dz), block(0, dz), block(0, dz), net.along_x(i))
 
-    for dz in (4, 3, -3, 2, -2, 1, -1):
+    for dz in (1, -1, 2, -2, 3, -3, 4):
         net.start(("Az", dz), block(0, 0), block(0, 0), net.along_z(dz))
     pass_on(0)
     yield
@@ -531,7 +531,7 @@
             column = (half * 2 + c) * BLK
             nets[half, net.x, net.z, c] = rounded[:, column : column + BLK]
 
-    take_turns(gather_z_first(net, nets.at[0]), gather_x_first(net, nets.at[1]))
+    take_turns(gather_x_first(net, nets.at[1]), gather_z_first(net, nets.at[0]))
 
     load_ptdf.wait()
     blocks = nets.reshape(2 * NX * NZ * 2, ROWS, BLK)

time: 89.6 us -> 90 us (level)
  no operation moved by 1% of the time
where the time goes in v5:
time: 90 us; the launch traced here: 89.8 us
  Pallas kernels  89.2 us (99%)
    pallas_call x1, Pallas kernels, network(): pl.pallas_call(network_kernel, name='network', out_shape=(jax.ShapeDtypeS...  86.7 us
    pallas_call x1, Pallas kernels, finish(): pl.pallas_call(finish_kernel, name='finish', out_shape=(jax.ShapeDtypeStr...  2.48 us

profile of v5, /device:TPU:1, one launch (start us, length us, event | category | flops | bytes accessed | tf_op | source)
XLA Modules:
  0.0 89.8 jit_solution(985086404333693784)
XLA Ops:
  0.6 86.7 %network.1 = (bf16[8,2,2,48,128]{4,3,2,1,0:T(8,128)(2,1)}, f32[2,12,4,768]{3,2,1,0:T(4,128)}) custom-call(s32[16]{0:T(128)} %counts.1, s32[16]{0:T(128)} %gen_bus.1, s32[6,16]{1,0:T(8,128)} %pattern.1, s32[3,16,512]{2,1,0:T(8,128)} %bitcast.9, f32[16,512]{1,0:T(8,128)} %level.1, f32[16,512]{1,0:T(8,128)} %cost.1, f32[12,32,512]{2,1,0:T(8,128)} %bitcast.6, ...), custom_call_target="tpu_custom_call" | custom-call | tf_op jit(solution)/shard_map/network/pallas_call | solution.py:602
  87.3 2.5 %finish.1 = (f32[12,32,512]{2,1,0:T(8,128)}, f32[2,12,4,768]{3,2,1,0:T(4,128)}) custom-call(bf16[8,2,2,48,128]{4,3,2,1,0:T(8,128)(2,1)} %get-tuple-element.6.finals, f32[12,32,512]{2,1,0:T(8,128)} %bitcast.7, f32[2,12,4,768]{3,2,1,0:T(4,128)} %get-tuple-element.7.mult), custom_call_target="tpu_custom_call" | custom-call | tf_op jit(solution)/shard_map/finish/pallas_call | solution.py:657
